TPU v7x, 128 devices: a whole 4x4x4 slice. The times are simulated.
128 devices in a mesh: line: 16 (over y, x), col: 8 (over z, core).
Axes of the slice: x: 4, y: 4, z: 4, core: 2. Of those that a mesh axis runs over, the one named last changes fastest.
Arguments:
- fields: float32 [4, 512, 64, 512], P(None, 'line', 'col'), may hold values from -4 to 4
- viscosity: float32 [512, 64, 512], P('line', 'col'), may hold values from 0.5 to 2
Outputs:
- updated: float32 [4, 512, 64, 512], P(None, 'line', 'col')
All inputs are finite; a program needn't handle non-finite values.
Results may differ from a plain program's by a relative error of at most 0.0003.
Values sent between devices are 32-bit elements; how exact they have to be, the bound alone decides.
A program may use at most 64 MiB of HBM per device.

v0:
```python
import jax
import jax.numpy as jnp
from jax import lax
from jax.sharding import PartitionSpec as P

STIFF = 3072


THERMAL_RATIO = 0.8
CROSS_RATE = 0.2
ADVECTION = 0.25
BUOYANCY = 2.0


def padded_2(block, sides, width, periodic):
    for axis, dim in sides:
        count = lax.axis_size(axis)
        forward = [(i, i + 1) for i in range(count - 1)]
        if periodic:
            forward.append((count - 1, 0))
        backward = [(target, source) for source, target in forward]
        low = lax.ppermute(
            lax.slice_in_dim(block, block.shape[dim] - width, None, axis=dim), axis, forward
        )
        high = lax.ppermute(lax.slice_in_dim(block, 0, width, axis=dim), axis, backward)
        block = jnp.concatenate([low, block, high], axis=dim)
    return block


def earlier(values, stride, along):
    length = values.shape[along]
    widths = [(0, 0)] * values.ndim
    widths[along] = (stride, 0)
    return lax.slice_in_dim(jnp.pad(values, widths), 0, length, axis=along)


def later(values, stride, along):
    length = values.shape[along]
    widths = [(0, 0)] * values.ndim
    widths[along] = (0, stride)
    return lax.slice_in_dim(jnp.pad(values, widths), stride, length + stride, axis=along)


def difference(padded, field, visc, along):
    length = field.shape[along]
    shifted_next = lax.slice_in_dim(padded, 2, length + 2, axis=along)
    shifted_prev = lax.slice_in_dim(padded, 0, length, axis=along)
    face_next = 0.5 * (visc + shifted_next[4:])
    face_prev = 0.5 * (visc + shifted_prev[4:])
    diffusion = face_next * (shifted_next[:4] - field) - face_prev * (field - shifted_prev[:4])
    central = 0.5 * (shifted_next[:4] - shifted_prev[:4])
    return (diffusion, central, face_prev, face_next)


def cyclic_reduce(sub_diag, super_diag, sources):
    length = sub_diag.shape[0]
    stride = 1
    for level in range((length - 1).bit_length()):
        sub_prev = earlier(sub_diag, stride, 0)
        super_prev = earlier(super_diag, stride, 0)
        sub_next = later(sub_diag, stride, 0)
        super_next = later(super_diag, stride, 0)
        source_prev = earlier(sources, stride, 1)
        source_next = later(sources, stride, 1)
        divisor = 1.0 - sub_diag * super_prev - super_diag * sub_next
        sources = (sources - sub_diag * source_prev - super_diag * source_next) / divisor
        new_sub = -(sub_diag * sub_prev) / divisor
        new_super = -(super_diag * super_next) / divisor
        sub_diag, super_diag = (new_sub, new_super)
        stride = stride * 2
    return sources


def local_solve(rate, face_prev, face_next, source):
    low_side = rate * face_prev
    high_side = rate * face_next
    diagonal = 1.0 + low_side + high_side
    sub_diag = -low_side / diagonal
    super_diag = -high_side / diagonal
    row_index = lax.broadcasted_iota(jnp.int32, sub_diag.shape, 0)
    last_row = sub_diag.shape[0] - 1
    spike_left = jnp.where(row_index == 0, -sub_diag, 0.0)
    spike_right = jnp.where(row_index == last_row, -super_diag, 0.0)
    sub_diag = jnp.where(row_index == 0, 0.0, sub_diag)
    super_diag = jnp.where(row_index == last_row, 0.0, super_diag)
    sources = jnp.concatenate([source / diagonal, spike_left[None], spike_right[None]], axis=0)
    return cyclic_reduce(sub_diag, super_diag, sources)


def per_field(pair):
    return jnp.concatenate([jnp.broadcast_to(pair[0:1], (3,) + pair.shape[1:]), pair[1:2]], axis=0)


def settle(coefficients):
    start_part = coefficients[0:4]
    end_part = coefficients[4:8]
    left_first = per_field(coefficients[8:10])
    left_last = per_field(coefficients[10:12])
    right_first = per_field(coefficients[12:14])
    right_last = per_field(coefficients[14:16])
    members = coefficients.shape[1]
    zeros_row = jnp.zeros_like(start_part[:, 0])
    carry_off, carry_gain = (zeros_row, zeros_row)
    first_off, first_gain, last_off, last_gain = ([], [], [], [])
    for member in range(members):
        divisor = 1.0 - left_first[:, member] * carry_gain
        offset = (start_part[:, member] + left_first[:, member] * carry_off) / divisor
        slope_first = right_first[:, member] / divisor
        carry_off = (
            end_part[:, member]
            + left_last[:, member] * carry_off
            + left_last[:, member] * carry_gain * offset
        )
        carry_gain = left_last[:, member] * carry_gain * slope_first + right_last[:, member]
        first_off.append(offset)
        first_gain.append(slope_first)
        last_off.append(carry_off)
        last_gain.append(carry_gain)
    firsts = [zeros_row] * members
    lasts = [zeros_row] * members
    following = zeros_row
    for member in reversed(range(members)):
        firsts[member] = first_off[member] + first_gain[member] * following
        lasts[member] = last_off[member] + last_gain[member] * following
        following = firsts[member]
    from_left = [zeros_row] + lasts[:-1]
    from_right = firsts[1:] + [zeros_row]
    return jnp.stack([jnp.stack(from_left, axis=1), jnp.stack(from_right, axis=1)])


def local(fields, viscosity):
    stacked = jnp.concatenate([fields, viscosity[None]], axis=0)
    padded_x = padded_2(stacked, (("line", 1),), 1, False)
    padded_y = padded_2(stacked, (("col", 2),), 1, True)
    padded_z = jnp.pad(stacked, ((0, 0), (0, 0), (0, 0), (1, 1)))
    visc = viscosity[None]
    _, central_x, face_prev, face_next = difference(padded_x, fields, visc, 1)
    along_y, central_y, _, _ = difference(padded_y, fields, visc, 2)
    along_z, central_z, _, _ = difference(padded_z, fields, visc, 3)
    transport = fields[0:1] * central_x + fields[1:2] * central_y + fields[2:3] * central_z
    scaling = jnp.array([1.0, 1.0, 1.0, THERMAL_RATIO], jnp.float32).reshape(4, 1, 1, 1)
    source = (
        fields + scaling * (CROSS_RATE * along_y + CROSS_RATE * along_z) - ADVECTION * transport
    )
    source = source.at[2].add(BUOYANCY * fields[3])
    velocity = local_solve(STIFF * 1.0, face_prev[0], face_next[0], source[:3])
    thermal = local_solve(STIFF * THERMAL_RATIO, face_prev[0], face_next[0], source[3:])
    partial_value = jnp.concatenate([velocity[:3], thermal[:1]], axis=0)
    coefficients = jnp.concatenate(
        [
            partial_value[:, 0],
            partial_value[:, -1],
            jnp.stack([velocity[3, 0], thermal[1, 0]]),
            jnp.stack([velocity[3, -1], thermal[1, -1]]),
            jnp.stack([velocity[4, 0], thermal[2, 0]]),
            jnp.stack([velocity[4, -1], thermal[2, -1]]),
        ],
        axis=0,
    )
    plane_shape = coefficients.shape[1:]
    coefficients = coefficients.reshape(16, 1, -1)
    columns = coefficients.shape[2]
    line_count = lax.axis_size("line")
    blocks = coefficients.reshape(16, 1, line_count, columns // line_count)
    swapped = settle(lax.all_to_all(blocks, "line", split_axis=2, concat_axis=1, tiled=True))
    returned = lax.all_to_all(swapped, "line", split_axis=2, concat_axis=3, tiled=True)
    own_bounds = returned[:, :, 0].reshape(2, 4, columns)
    bound_left = own_bounds[0].reshape((4,) + plane_shape)
    bound_right = own_bounds[1].reshape((4,) + plane_shape)
    velocity_new = (
        velocity[:3] + velocity[3:4] * bound_left[:3, None] + velocity[4:5] * bound_right[:3, None]
    )
    thermal_new = (
        thermal[0:1] + thermal[1:2] * bound_left[3:, None] + thermal[2:3] * bound_right[3:, None]
    )
    return jnp.concatenate([velocity_new, thermal_new], axis=0)


def solution(mesh):
    return jax.shard_map(
        local,
        mesh=mesh,
        in_specs=(P(None, "line", "col", None), P("line", "col", None)),
        out_specs=P(None, "line", "col", None),
        check_vma=False,
    )
```

profile of v0, /device:TPU:0, one launch (start us, length us, event | category | flops | bytes accessed | tf_op | source)
XLA Modules:
  0.0 70.3 jit_solution(1818091534499843422)
XLA Ops:
  0.0 1.0 %fusion.171 = (f32[5,1,8,512]{3,2,1,0:T(8,128)S(1)}, f32[5,1,8,512]{3,2,1,0:T(8,128)S(1)}) fusion(f32[4,32,8,512]{3,2,1,0:T(8,128)} %param.5, f32[1,32,8,512]{3,2,1,0:T(8,128)} %bitcast.103), kind=kLoop, calls=%fused_computation.386 | loop fusion | flops 40960 | bytes 2785280 | tf_op jit(solution)/shard_map/concatenate | solution.py:132
  1.0 1.3 %collective-permute-start.2 = (f32[5,1,8,512]{3,2,1,0:T(8,128)S(1)}, f32[5,1,8,512]{3,2,1,0:T(8,128)S(1)}, u32[]{:S(2)}, u32[]{:S(2)}) collective-permute-start(f32[5,1,8,512]{3,2,1,0:T(8,128)S(1)} %get-tuple-element.125), channel_id=1, source_target_pairs={{8,0},{16,8},{24,16},{32,24},{40,32},{48,40},{56,48},{64,56},{72,6... | collective-permute-start | bytes 245768 | tf_op jit(solution)/shard_map/ppermute | solution.py:25
  2.3 4.6 %collective-permute-start.3 = (f32[5,1,8,512]{3,2,1,0:T(8,128)S(1)}, f32[5,1,8,512]{3,2,1,0:T(8,128)S(1)}, u32[]{:S(2)}, u32[]{:S(2)}) collective-permute-start(f32[5,1,8,512]{3,2,1,0:T(8,128)S(1)} %get-tuple-element.124), channel_id=1, source_target_pairs={{0,8},{8,16},{16,24},{24,32},{32,40},{40,48},{48,56},{56,64},{64,7... | collective-permute-start | bytes 245768 | tf_op jit(solution)/shard_map/ppermute | solution.py:22
  6.9 0.4 fusion.167
  7.3 3.0 %collective-permute-start = (f32[5,32,1,512]{3,2,1,0:T(1,128)S(1)}, f32[5,32,1,512]{3,2,1,0:T(1,128)S(1)}, u32[]{:S(2)}, u32[]{:S(2)}) collective-permute-start(f32[5,32,1,512]{3,2,1,0:T(1,128)S(1)} %get-tuple-element.120), channel_id=1, source_target_pairs={{1,0},{2,1},{3,2},{4,3},{5,4},{6,5},{7,6},{0,7},{9,8},{10,9},{11,1... | collective-permute-start | bytes 983048 | tf_op jit(solution)/shard_map/ppermute | solution.py:25
  10.4 0.4 pad_maximum_fusion
  10.8 0.3 fusion.156
  11.1 0.8 %pad_maximum_fusion.1 = (f32[5,33,8,512]{3,2,1,0:T(8,128)S(1)}, f32[5,33,8,512]{3,2,1,0:T(8,128)S(1)}) fusion(f32[5,1,8,512]{3,2,1,0:T(8,128)S(1)} %collective-permute-done.2, f32[1,32,8,512]{3,2,1,0:T(8,128)S(1)} %bitcast.106, f32[4,32,8,512]{3,2,1,0:T(8,128)S(1)} %copy-done, f32[5,1,8,512]{3,2,1,0:T(8,128)S(1)} %collective-permute-done.3), kind=kLoop, calls=%fused_computation.21 | loop fusion | flops 2703360 | bytes 8192000 | tf_op jit(solution)/shard_map/concatenate | solution.py:26
  12.0 3.0 %collective-permute-done = f32[5,32,1,512]{3,2,1,0:T(1,128)S(1)} collective-permute-done((f32[5,32,1,512]{3,2,1,0:T(1,128)S(1)}, f32[5,32,1,512]{3,2,1,0:T(1,128)S(1)}, u32[]{:S(2)}, u32[]{:S(2)}) %collective-permute-start) | collective-permute-done | bytes 327712 | tf_op jit(solution)/shard_map/ppermute | solution.py:25
  15.0 3.1 %collective-permute-done.1 = f32[5,32,1,512]{3,2,1,0:T(1,128)S(1)} collective-permute-done((f32[5,32,1,512]{3,2,1,0:T(1,128)S(1)}, f32[5,32,1,512]{3,2,1,0:T(1,128)S(1)}, u32[]{:S(2)}, u32[]{:S(2)}) %collective-permute-start.1) | collective-permute-done | bytes 327712 | tf_op jit(solution)/shard_map/ppermute | solution.py:22
  18.1 0.7 select_bitcast_fusion.3
  18.8 3.0 %fusion.29 = f32[4,32,8,512]{3,2,1,0:T(8,128)S(1)} fusion(f32[5,33,8,512]{3,2,1,0:T(8,128)S(1)} %get-tuple-element.123, f32[5,33,8,512]{3,2,1,0:T(8,128)S(1)} %get-tuple-element.122, f32[1,32,8,512]{3,2,1,0:T(8,128)S(1)} %bitcast.108, f32[4,32,8,512]{3,2,1,0:T(8,128)S(1)} %copy-done, f32[5,32,1,512]{3,2,1,0:T(1,128)S(1)} %collective-permute-done.1, ...), kind=kLoop, calls=%fused_computation.58 | loop fusion | flops 14680064 | bytes 15859728 | tf_op jit(solution)/shard_map/sub | solution.py:143
  21.8 0.2 fusion.162
  22.0 0.4 bitcast_select_fusion.3
  22.4 0.5 select_bitcast_fusion.2
  22.9 0.2 fusion.85
  23.1 0.2 fusion.75
  23.2 0.2 fusion.72
  23.5 0.2 fusion.95
  23.9 0.8 %fusion.44 = (f32[3,32,8,512]{3,2,1,0:T(8,128)S(1)}, f32[3,32,8,512]{3,2,1,0:T(8,128)S(1)}) fusion(f32[3,32,8,512]{3,2,1,0:T(8,128)S(1)} %pad_maximum_fusion.8, f32[32,8,512]{2,1,0:T(8,128)S(1)} %get-tuple-element.109, f32[32,8,512]{2,1,0:T(8,128)S(1)} %get-tuple-element.137, f32[32,8,512]{2,1,0:T(8,128)S(1)} %get-tuple-element.146, ...), kind=kLoop, calls=%fused_computation.86 | loop fusion | flops 2359296 | bytes 8388608 | tf_op jit(solution)/shard_map/div | solution.py:66
  24.7 0.3 pad_maximum_fusion.2
  25.0 0.6 fusion.3
  25.6 0.6 fusion.8
  26.2 0.2 fusion.115
  26.5 0.6 fusion.13
  27.1 0.2 fusion.135
  27.4 0.8 %fusion.18 = f32[5,32,8,512]{3,2,1,0:T(8,128)S(1)} fusion(f32[5,32,8,512]{3,2,1,0:T(8,128)S(1)} %fusion.13, f32[32,8,512]{2,1,0:T(8,128)S(1)} %get-tuple-element.92, f32[32,8,512]{2,1,0:T(8,128)S(1)} %get-tuple-element.93, f32[32,8,512]{2,1,0:T(8,128)S(1)} %fusion.112), kind=kLoop, calls=%fused_computation.43 | loop fusion | flops 3276800 | bytes 6815744 | tf_op jit(solution)/shard_map/div | solution.py:66
  28.3 0.8 %fusion.23 = f32[5,32,8,512]{3,2,1,0:T(8,128)S(1)} fusion(f32[5,32,8,512]{3,2,1,0:T(8,128)S(1)} %fusion.18, f32[32,8,512]{2,1,0:T(8,128)S(1)} %fusion.148, f32[32,8,512]{2,1,0:T(8,128)S(1)} %get-tuple-element.91, f32[32,8,512]{2,1,0:T(8,128)S(1)} %fusion.132), kind=kLoop, calls=%fused_computation.48 | loop fusion | flops 3276800 | bytes 6815744 | tf_op jit(solution)/shard_map/div | solution.py:66
  29.3 1.3 %copy-done.2 = f32[5,32,8,512]{3,2,1,0:T(8,128)} copy-done((f32[5,32,8,512]{3,2,1,0:T(8,128)}, f32[5,32,8,512]{3,2,1,0:T(8,128)S(1)}, u32[]{:S(2)}) %copy-start.2) | copy-done | bytes 2621464
  30.7 0.4 fusion.49
  31.4 0.4 fusion.54
  31.8 0.2 fusion.145
  32.1 0.4 fusion.59
  32.7 0.4 fusion.64
  33.2 0.9 %slice-done = f32[3,32,8,512]{3,2,1,0:T(8,128)S(1)} async-done(((f32[5,32,8,512]{3,2,1,0:T(8,128)}), f32[3,32,8,512]{3,2,1,0:T(8,128)S(1)}, s32[]{:S(2)}) %slice-start) | async-done | bytes 1572888 | tf_op jit(solution)/shard_map/slice | solution.py:171
  34.1 0.2 copy-done.4
  34.5 0.9 %copy.22 = f32[16,1,16,256]{3,0,1,2:T(8,128)} copy(f32[16,1,16,256]{3,2,0,1:T(8,128)S(1)} %constant_dynamic-update-slice_fusion) | data formatting | bytes 524288 | tf_op jit(solution)/shard_map/concatenate | solution.py:149
  35.4 9.1 %all-to-all-start = ((f32[16,1,16,256]{3,0,1,2:T(8,128)}), f32[16,1,16,256]{3,0,1,2:T(8,128)S(1)}, u32[]{:S(2)}, u32[]{:S(2)}) async-start(f32[16,1,16,256]{3,0,1,2:T(8,128)} %copy.22), calls=%async_computation | async-start | bytes 524288 | tf_op jit(solution)/shard_map/all_to_all | solution.py:165
  44.5 8.7 %all-to-all-done = f32[16,1,16,256]{3,0,1,2:T(8,128)S(1)} async-done(((f32[16,1,16,256]{3,0,1,2:T(8,128)}), f32[16,1,16,256]{3,0,1,2:T(8,128)S(1)}, u32[]{:S(2)}, u32[]{:S(2)}) %all-to-all-start) | async-done | bytes 262176 | tf_op jit(solution)/shard_map/all_to_all | solution.py:165
  53.5 0.2 fusion.216
  53.7 0.3 constant_dynamic-update-slice_fusion.24
  54.5 0.7 copy.28
  55.2 3.5 %all-to-all-start.1 = ((f32[2,4,16,1,256]{4,1,3,0,2:T(4,128)}), f32[2,4,16,1,256]{4,1,3,0,2:T(4,128)S(1)}, u32[]{:S(2)}, u32[]{:S(2)}) async-start(f32[2,4,16,1,256]{4,1,3,0,2:T(4,128)} %copy.28), calls=%async_computation.1 | async-start | bytes 262144 | tf_op jit(solution)/shard_map/all_to_all | solution.py:166
  58.7 0.9 %slice_bitcast_fusion.1 = (f32[32,8,512]{2,1,0:T(8,128)S(1)}, f32[32,8,512]{2,1,0:T(8,128)}) fusion(f32[5,32,8,512]{3,2,1,0:T(8,128)S(1)} %copy-done.3), kind=kLoop, calls=%fused_computation.247 | loop fusion | bytes 2097152 | tf_op jit(solution)/shard_map/mul | solution.py:171
  59.6 7.1 %all-to-all-done.1 = f32[2,4,16,1,256]{4,1,3,0,2:T(4,128)S(1)} async-done(((f32[2,4,16,1,256]{4,1,3,0,2:T(4,128)}), f32[2,4,16,1,256]{4,1,3,0,2:T(4,128)S(1)}, u32[]{:S(2)}, u32[]{:S(2)}) %all-to-all-start.1) | async-done | bytes 131104 | tf_op jit(solution)/shard_map/all_to_all | solution.py:166
  66.9 1.6 %fusion.160 = f32[1,32,8,512]{3,2,1,0:T(8,128)S(1)} fusion(f32[3,32,8,512]{3,2,1,0:T(8,128)} %copy-done.4, f32[8,512]{1,0:T(8,128)S(1)} %mul.7152, f32[8,512]{1,0:T(8,128)S(1)} %mul.7149), kind=kLoop, calls=%fused_computation.242 | loop fusion | flops 524288 | bytes 2129920 | tf_op jit(solution)/shard_map/add | solution.py:174
  68.5 0.3 multiply_add_fusion
  68.8 1.5 %pad_maximum_fusion.7 = f32[4,32,8,512]{3,2,1,0:T(8,128)} fusion(f32[1,32,8,512]{3,2,1,0:T(8,128)S(1)} %fusion.160, f32[3,32,8,512]{3,2,1,0:T(8,128)S(1)} %multiply_add_fusion), kind=kLoop, calls=%fused_computation.74 | loop fusion | flops 524288 | bytes 4194304 | tf_op jit(solution)/shard_map/concatenate | solution.py:176
  (105 shorter events, 2.2 us)
Async XLA Ops:
  0.0 6.9 %copy-start.1 = (f32[32,8,512]{2,1,0:T(8,128)S(1)}, f32[32,8,512]{2,1,0:T(8,128)}, u32[]{:S(2)}) copy-start(f32[32,8,512]{2,1,0:T(8,128)} %param.6) | copy-start | bytes 1572868
  0.0 6.9 %copy-start = (f32[4,32,8,512]{3,2,1,0:T(8,128)S(1)}, f32[4,32,8,512]{3,2,1,0:T(8,128)}, u32[]{:S(2)}) copy-start(f32[4,32,8,512]{3,2,1,0:T(8,128)} %param.5) | copy-start | bytes 6291460
  1.0 10.1 %collective-permute-start.2 = (f32[5,1,8,512]{3,2,1,0:T(8,128)S(1)}, f32[5,1,8,512]{3,2,1,0:T(8,128)S(1)}, u32[]{:S(2)}, u32[]{:S(2)}) collective-permute-start(f32[5,1,8,512]{3,2,1,0:T(8,128)S(1)} %get-tuple-element.125), channel_id=1, source_target_pairs={{8,0},{16,8},{24,16},{32,24},{40,32},{48,40},{56,48},{64,56},{72,6... | collective-permute-start | bytes 245768 | tf_op jit(solution)/shard_map/ppermute | solution.py:25
  2.3 8.8 %collective-permute-start.3 = (f32[5,1,8,512]{3,2,1,0:T(8,128)S(1)}, f32[5,1,8,512]{3,2,1,0:T(8,128)S(1)}, u32[]{:S(2)}, u32[]{:S(2)}) collective-permute-start(f32[5,1,8,512]{3,2,1,0:T(8,128)S(1)} %get-tuple-element.124), channel_id=1, source_target_pairs={{0,8},{8,16},{16,24},{24,32},{32,40},{40,48},{48,56},{56,64},{64,7... | collective-permute-start | bytes 245768 | tf_op jit(solution)/shard_map/ppermute | solution.py:22
  7.3 7.6 %collective-permute-start = (f32[5,32,1,512]{3,2,1,0:T(1,128)S(1)}, f32[5,32,1,512]{3,2,1,0:T(1,128)S(1)}, u32[]{:S(2)}, u32[]{:S(2)}) collective-permute-start(f32[5,32,1,512]{3,2,1,0:T(1,128)S(1)} %get-tuple-element.120), channel_id=1, source_target_pairs={{1,0},{2,1},{3,2},{4,3},{5,4},{6,5},{7,6},{0,7},{9,8},{10,9},{11,1... | collective-permute-start | bytes 983048 | tf_op jit(solution)/shard_map/ppermute | solution.py:25
  10.4 7.7 %collective-permute-start.1 = (f32[5,32,1,512]{3,2,1,0:T(1,128)S(1)}, f32[5,32,1,512]{3,2,1,0:T(1,128)S(1)}, u32[]{:S(2)}, u32[]{:S(2)}) collective-permute-start(f32[5,32,1,512]{3,2,1,0:T(1,128)S(1)} %get-tuple-element.121), channel_id=1, source_target_pairs={{0,1},{1,2},{2,3},{3,4},{4,5},{5,6},{6,7},{7,0},{8,9},{9,10},{10,1... | collective-permute-start | bytes 983048 | tf_op jit(solution)/shard_map/ppermute | solution.py:22
  11.9 6.8 %copy-start.6 = (f32[4]{0:T(128)S(1)}, f32[4]{0:T(128)}, u32[]{:S(2)}) copy-start(f32[4]{0:T(128)} %constant.80.clone) | copy-start | bytes 52
  29.1 1.5 %copy-start.2 = (f32[5,32,8,512]{3,2,1,0:T(8,128)}, f32[5,32,8,512]{3,2,1,0:T(8,128)S(1)}, u32[]{:S(2)}) copy-start(f32[5,32,8,512]{3,2,1,0:T(8,128)S(1)} %fusion.23) | copy-start | bytes 7864324
  32.7 1.4 %slice-start = ((f32[5,32,8,512]{3,2,1,0:T(8,128)}), f32[3,32,8,512]{3,2,1,0:T(8,128)S(1)}, s32[]{:S(2)}) async-start(f32[5,32,8,512]{3,2,1,0:T(8,128)} %copy-done.2), calls=%async_computation.2 | async-start | bytes 3145728 | tf_op jit(solution)/shard_map/slice | solution.py:171
  33.1 1.1 %copy-start.4 = (f32[3,32,8,512]{3,2,1,0:T(8,128)}, f32[3,32,8,512]{3,2,1,0:T(8,128)S(1)}, u32[]{:S(2)}) copy-start(f32[3,32,8,512]{3,2,1,0:T(8,128)S(1)} %fusion.64) | copy-start | bytes 4718596
  35.4 23.3 %copy-start.3 = (f32[5,32,8,512]{3,2,1,0:T(8,128)S(1)}, f32[5,32,8,512]{3,2,1,0:T(8,128)}, u32[]{:S(2)}) copy-start(f32[5,32,8,512]{3,2,1,0:T(8,128)} %copy-done.2) | copy-start | bytes 7864324
  35.4 17.8 %all-to-all-start = ((f32[16,1,16,256]{3,0,1,2:T(8,128)}), f32[16,1,16,256]{3,0,1,2:T(8,128)S(1)}, u32[]{:S(2)}, u32[]{:S(2)}) async-start(f32[16,1,16,256]{3,0,1,2:T(8,128)} %copy.22), calls=%async_computation | async-start | bytes 524288 | tf_op jit(solution)/shard_map/all_to_all | solution.py:165
  55.2 11.5 %all-to-all-start.1 = ((f32[2,4,16,1,256]{4,1,3,0,2:T(4,128)}), f32[2,4,16,1,256]{4,1,3,0,2:T(4,128)S(1)}, u32[]{:S(2)}, u32[]{:S(2)}) async-start(f32[2,4,16,1,256]{4,1,3,0,2:T(4,128)} %copy.28), calls=%async_computation.1 | async-start | bytes 262144 | tf_op jit(solution)/shard_map/all_to_all | solution.py:166
  66.9 1.6 %copy-start.5 = (f32[32,8,512]{2,1,0:T(8,128)S(1)}, f32[32,8,512]{2,1,0:T(8,128)}, u32[]{:S(2)}) copy-start(f32[32,8,512]{2,1,0:T(8,128)} %get-tuple-element.113) | copy-start | bytes 1572868
where the time goes:
time: 70.7 us; the launch traced here: 70.3 us
  waiting for transfers between devices  21.9 us (31%)
  starting transfers between devices  21.5 us (30%)
  other arithmetic  20.6 us (29%)
  local copies, waits for them, and re-layouts  5.46 us (8%)
  between operations  0.86 us (1%)
    all_to_all x1, starting transfers between devices, local(): lax.all_to_all(blocks, 'line', split_axis=2, concat_axis=1, tiled=True)  9.14 us
    all_to_all x1, waiting for transfers between devices, local(): lax.all_to_all(blocks, 'line', split_axis=2, concat_axis=1, tiled=True)  8.68 us
    all_to_all x1, waiting for transfers between devices, local(): lax.all_to_all(swapped, 'line', split_axis=2, concat_axis=3, tiled=True)  7.08 us
    div x10, other arithmetic, cyclic_reduce(): (sources - sub_diag * source_prev - super_diag * source_next) / divisor  5.83 us
    ppermute x2, starting transfers between devices, padded_2(): lax.ppermute(lax.slice_in_dim(block, block.shape[dim] - width, None, axis...  4.55 us
    ppermute x2, starting transfers between devices, padded_2(): lax.ppermute(lax.slice_in_dim(block, 0, width, axis=dim), axis, backward)  4.33 us
    all_to_all x1, starting transfers between devices, local(): lax.all_to_all(swapped, 'line', split_axis=2, concat_axis=3, tiled=True)  3.51 us
    ppermute x2, waiting for transfers between devices, padded_2(): lax.ppermute(lax.slice_in_dim(block, block.shape[dim] - width, None, axis...  3.12 us
  transfers between devices with their start and end apart: 6, of which 4 were waited for; matrix products, arithmetic and copies ran while one was open for 4% of the time, Pallas kernels for 0%

commit v1 on v0

v1 whole, which is shorter than its diff:
```python
import functools

import jax
import jax.numpy as jnp
from jax import lax
from jax.experimental import pallas as pl
from jax.experimental.pallas import tpu as pltpu
from jax.sharding import PartitionSpec as P

STIFF = 3072.0
THERMAL_RATIO = 0.8
CROSS_RATE = 0.2
ADVECTION = 0.25
BUOYANCY = 2.0
MESH = pl.DeviceIdType.MESH
LANES = 128
SIDE = 4


def rates(q):
    return 0.5 * STIFF * (1.0 if q == 0 else THERMAL_RATIO)


def main_kernel(
    lines, cols, rows, chunks,
    f_hbm, v_hbm,
    y_out, m_out, w_out, b_out,
    fv, src, rec, mass, halo_out, halo_in,
    mat_out, mat_in, rhs_out, rhs_in, sep, bounds, pivots,
    load_sem, x_send, x_recv, y_send, y_recv,
    mat_send, mat_recv, rhs_send, rhs_recv, sep_send, sep_recv, plane_sem,
):
    me = lax.axis_index("line")
    col = lax.axis_index("col")
    right, left = lax.rem(me + 1, lines), lax.rem(me + lines - 1, lines)
    above, below = lax.rem(col + 1, cols), lax.rem(col + cols - 1, cols)
    row_of, place = me // SIDE, lax.rem(me, SIDE)
    last = rows - 1

    barrier = pltpu.get_barrier_semaphore()
    row_peers = [row_of * SIDE + lax.rem(place + d, SIDE) for d in range(1, SIDE)]
    column_peers = [lax.rem(row_of + d, lines // SIDE) * SIDE + place for d in range(1, lines // SIDE)]
    greeted = [{"line": p} for p in row_peers + column_peers + [right, left]]
    greeted += [{"col": above}, {"col": below}]
    for peer in greeted:
        pl.semaphore_signal(barrier, inc=1, device_id=peer, device_id_type=MESH)

    loads = []
    for c in range(chunks):
        lanes = pl.ds(c * LANES, LANES)
        own = pl.ds(1, rows)
        loads.append((
            pltpu.make_async_copy(v_hbm.at[:, :, lanes], fv.at[4, c, own], load_sem.at[c, 0]),
            pltpu.make_async_copy(f_hbm.at[:, :, :, lanes], fv.at[pl.ds(0, 4), c, own], load_sem.at[c, 1]),
        ))
    for pair in loads:
        pair[0].start()
        pair[1].start()

    for c in range(chunks):
        loads[c][0].wait()
        loads[c][1].wait()
        for a in range(5):
            for side, y in ((0, 7), (1, 0)):
                for g in range(0, rows, 8):
                    halo_out[side, c, a, g : g + 8, :] = fv[a, c, 1 + g : 9 + g, y, :]

    pl.semaphore_wait(barrier, len(greeted))

    to_right = pltpu.make_async_remote_copy(
        fv.at[:, :, rows], fv.at[:, :, 0], x_send.at[0], x_recv.at[0],
        device_id={"line": right}, device_id_type=MESH)
    to_left = pltpu.make_async_remote_copy(
        fv.at[pl.ds(0, 4), :, 1], fv.at[pl.ds(0, 4), :, rows + 1], x_send.at[1], x_recv.at[1],
        device_id={"line": left}, device_id_type=MESH)
    to_right.start()
    to_left.start()
    y_copies = []
    for c in range(chunks):
        pair = []
        for side, peer in ((0, above), (1, below)):
            copy = pltpu.make_async_remote_copy(
                halo_out.at[side, c], halo_in.at[side, c], y_send.at[side, c], y_recv.at[side, c],
                device_id={"col": peer}, device_id_type=MESH)
            copy.start()
            pair.append(copy)
        y_copies.append(pair)
    for peer in column_peers:
        pl.semaphore_signal(plane_sem, inc=1, device_id={"line": peer}, device_id_type=MESH)

    def matrix_step(k, carry):
        new = []
        for c in range(chunks):
            total = fv[4, c, k + 1] + fv[4, c, k]
            for q in range(2):
                h, e, mass_right = carry[2 * c + q]
                a = rates(q) * total
                r = 1.0 / (a + (h + e))
                m = a * r
                w = e * r
                rec[q, c, k] = r
                m_out[q, c, k] = m
                w_out[q, c, k] = w
                new.append((1.0 + m * h, m * e, mass_right + w * h))
        return tuple(new)

    start = []
    for c in range(chunks):
        total = fv[4, c, rows] + fv[4, c, rows - 1]
        for q in range(2):
            a = rates(q) * total
            start.append((jnp.ones_like(a), a, jnp.zeros_like(a)))
    state = lax.fori_loop(0, last - 1, lambda i, s: matrix_step(last - 1 - i, s), tuple(start))
    for c in range(chunks):
        for q in range(2):
            for n in range(3):
                mass[q, c, n] = state[2 * c + q][n]

    shape = (8, LANES)
    lane = lax.broadcasted_iota(jnp.int32, shape, 1)
    level = lax.broadcasted_iota(jnp.int32, shape, 0)
    z_first, z_last = lane == 0, lane == LANES - 1
    y_first, y_last = level == 0, level == 7

    def z_pair(values):
        ahead = [pltpu.roll(x, LANES - 1, 1) for x in values] + [jnp.zeros(shape, jnp.float32)]
        behind = [jnp.zeros(shape, jnp.float32)] + [pltpu.roll(x, 1, 1) for x in values]
        z_next = [jnp.where(z_last, ahead[c + 1], ahead[c]) for c in range(chunks)]
        z_prev = [jnp.where(z_first, behind[c], behind[c + 1]) for c in range(chunks)]
        return z_next, z_prev

    def source_row(p):
        visc = [fv[4, c, p] for c in range(chunks)]
        z_next, z_prev = z_pair(visc)
        half = 0.5 * CROSS_RATE
        az_next = [half * (visc[c] + z_next[c]) for c in range(chunks)]
        az_prev = [half * (visc[c] + z_prev[c]) for c in range(chunks)]
        ay_next = [jnp.where(y_last, 0.0, half * (visc[c] + pltpu.roll(visc[c], 7, 0))) for c in range(chunks)]
        ay_prev = [jnp.where(y_first, 0.0, half * (visc[c] + pltpu.roll(visc[c], 1, 0))) for c in range(chunks)]
        speed = [[(0.5 * ADVECTION) * fv[a, c, p] for c in range(chunks)] for a in range(3)]
        for a in range(4):
            own = [fv[a, c, p] for c in range(chunks)]
            z_next, z_prev = z_pair(own)
            for c in range(chunks):
                f = own[c]
                y_next = jnp.where(y_last, 0.0, pltpu.roll(f, 7, 0))
                y_prev = jnp.where(y_first, 0.0, pltpu.roll(f, 1, 0))
                spread = az_next[c] * (z_next[c] - f) - az_prev[c] * (f - z_prev[c])
                spread += ay_next[c] * (y_next - f) - ay_prev[c] * (f - y_prev)
                carried = speed[0][c] * (fv[a, c, p + 1] - fv[a, c, p - 1])
                carried += speed[1][c] * (y_next - y_prev) + speed[2][c] * (z_next[c] - z_prev[c])
                total = f + (THERMAL_RATIO * spread if a == 3 else spread) - carried
                if a == 2:
                    total += BUOYANCY * fv[3, c, p]
                src[a, c, p - 1] = total

    def source_step(p, nothing):
        source_row(p)
        return nothing

    lax.fori_loop(2, rows, source_step, 0)

    to_right.wait_recv()
    to_left.wait_recv()

    @pl.when(me == 0)
    def _():
        fv[:, :, 0] = jnp.zeros((5, chunks) + shape, jnp.float32)

    @pl.when(me == lines - 1)
    def _():
        fv[0:4, :, rows + 1] = jnp.zeros((4, chunks) + shape, jnp.float32)

    source_row(1)
    source_row(rows)

    at_end = jnp.where(me == lines - 1, 1.0, 0.0)
    for c in range(chunks):
        total = fv[4, c, 1] + fv[4, c, 0]
        wall = at_end * fv[4, c, rows]
        for q in range(2):
            h, e, mass_right = (mass[q, c, n] for n in range(3))
            a = rates(q) * total
            r = 1.0 / (a + (h + e))
            m = a * r
            w = e * r
            rec[q, c, 0] = r
            m_out[q, c, 0] = m
            w_out[q, c, 0] = w
            mat_out[c, q, 0] = m * e
            mat_out[c, q, 1] = m * h
            mat_out[c, q, 2] = 1.0 + mass_right + w * h + rates(q) * wall

    pl.semaphore_wait(plane_sem, len(column_peers))

    def mat_copy(owner):
        c, a = owner // 4, lax.rem(owner, 4)
        return pltpu.make_async_remote_copy(
            mat_out.at[c, a // 3], mat_in.at[me], mat_send.at[owner], mat_recv.at[me],
            device_id={"line": owner}, device_id_type=MESH)

    def mat_start(d, nothing):
        mat_copy(lax.rem(me + d, lines)).start()
        return nothing

    lax.fori_loop(1, lines, mat_start, 0)
    mat_in[me] = mat_out[me // 4, lax.rem(me, 4) // 3]

    edge = jnp.where(y_first | y_last, 0.5 * CROSS_RATE, 0.0)
    sign = jnp.where(y_last, -0.5 * ADVECTION, jnp.where(y_first, 0.5 * ADVECTION, 0.0))

    def rhs_copy(owner):
        return pltpu.make_async_remote_copy(
            rhs_out.at[owner], rhs_in.at[me], rhs_send.at[owner], rhs_recv.at[me],
            device_id={"line": owner}, device_id_type=MESH)

    for c in range(chunks):
        for copy in y_copies[c]:
            copy.wait_recv()

        def finished(k):
            def beyond(a):
                low = jnp.broadcast_to(halo_in[0, c, a, pl.ds(k, 1), :], shape)
                high = jnp.broadcast_to(halo_in[1, c, a, pl.ds(k, 1), :], shape)
                return jnp.where(y_last, high, low)

            face = edge * (fv[4, c, k + 1] + beyond(4))
            speed = sign * fv[1, c, k + 1]
            out = []
            for a in range(4):
                outer = beyond(a)
                spread = face * (outer - fv[a, c, k + 1])
                if a == 3:
                    spread = THERMAL_RATIO * spread
                out.append(src[a, c, k] + (spread + speed * outer))
            return out

        def rhs_step(i, carry):
            k = last - 1 - i
            given = finished(k)
            new = []
            for a in range(4):
                q = a // 3
                passed, gathered = carry[a]
                d = given[a] + passed
                y_out[a, c, k] = rec[q, c, k] * d
                new.append((m_out[q, c, k] * d, gathered + w_out[q, c, k] * d))
            return tuple(new)

        at_last = finished(last)
        zero = jnp.zeros(shape, jnp.float32)
        ends = lax.fori_loop(0, last, rhs_step, tuple((zero, at_last[a]) for a in range(4)))
        for a in range(4):
            rhs_out[4 * c + a, 0] = ends[a][0]
            rhs_out[4 * c + a, 1] = ends[a][1]

        for a in range(4):
            owner = 4 * c + a

            @pl.when(me != owner)
            def _(owner=owner):
                rhs_copy(owner).start()

    rhs_in[me] = rhs_out[me]

    def mat_wait(d, nothing):
        j = lax.rem(me + d, lines)
        pltpu.make_async_remote_copy(
            mat_out.at[0, 0], mat_in.at[j], mat_send.at[j], mat_recv.at[j],
            device_id={"line": j}, device_id_type=MESH).wait_recv()
        return nothing

    lax.fori_loop(1, lines, mat_wait, 0)

    def pivot_step(j, before):
        e = mat_in[j, 0]
        r = 1.0 / (e + before)
        m = e * r
        pivots[j, 0] = r
        pivots[j, 1] = m
        ahead = jnp.minimum(j + 1, lines - 1)
        own_mass = mat_in[j, 2] + jnp.where(j + 1 < lines, 1.0, 0.0) * mat_in[ahead, 1]
        return own_mass + m * before

    first = mat_in[0, 0] + (mat_in[0, 2] + mat_in[1, 1])
    final = lax.fori_loop(1, lines, pivot_step, first)
    final = 1.0 / final

    def rhs_wait(d, nothing):
        j = lax.rem(me + d, lines)
        pltpu.make_async_remote_copy(
            rhs_out.at[j], rhs_in.at[j], rhs_send.at[j], rhs_recv.at[j],
            device_id={"line": j}, device_id_type=MESH).wait_recv()
        return nothing

    lax.fori_loop(1, lines, rhs_wait, 0)
    given = [rhs_in[j, 1] + rhs_in[j + 1, 0] if j + 1 < lines else rhs_in[j, 1] for j in range(lines)]
    for j in range(1, lines):
        given[j] = given[j] + pivots[j, 1] * given[j - 1]
    value = final * given[lines - 1]
    sep[0] = jnp.zeros(shape, jnp.float32)
    sep[lines] = value
    for j in range(lines - 1, 0, -1):
        value = pivots[j, 0] * given[j - 1] + pivots[j, 1] * value
        sep[j] = value

    def sep_copy(j):
        return pltpu.make_async_remote_copy(
            sep.at[pl.ds(j, 2)], bounds.at[me], sep_send.at[j], sep_recv.at[me],
            device_id={"line": j}, device_id_type=MESH)

    def sep_start(d, nothing):
        sep_copy(lax.rem(me + d, lines)).start()
        return nothing

    lax.fori_loop(1, lines, sep_start, 0)
    bounds[me] = sep[pl.ds(me, 2)]

    to_right.wait_send()
    to_left.wait_send()
    for pair in y_copies:
        for copy in pair:
            copy.wait_send()
    for owner in range(lines):

        @pl.when(me != owner)
        def _(owner=owner):
            rhs_copy(owner).wait_send()

    def sent(d, nothing):
        j = lax.rem(me + d, lines)
        mat_copy(j).wait_send()
        sep_copy(j).wait_send()
        return nothing

    lax.fori_loop(1, lines, sent, 0)

    def sep_wait(d, nothing):
        j = lax.rem(me + d, lines)
        pltpu.make_async_remote_copy(
            sep.at[pl.ds(0, 2)], bounds.at[j], sep_send.at[j], sep_recv.at[j],
            device_id={"line": j}, device_id_type=MESH).wait_recv()
        return nothing

    lax.fori_loop(1, lines, sep_wait, 0)
    b_out[...] = bounds[...]


def back_kernel(rows, chunks, y, m, w, b, out, buf, sem):
    last = rows - 1
    copies = []
    for c in range(chunks):
        ends = [b[4 * c + a, 1] for a in range(4)]

        def step(k, before):
            new = []
            for a in range(4):
                q = a // 3
                u = y[a, c, k] + m[q, c, k] * before[a] + w[q, c, k] * ends[a]
                buf[a, c, k] = u
                new.append(u)
            return tuple(new)

        lax.fori_loop(0, last, step, tuple(b[4 * c + a, 0] for a in range(4)))
        for a in range(4):
            buf[a, c, last] = ends[a]
        copy = pltpu.make_async_copy(buf.at[:, c], out.at[:, :, :, pl.ds(c * LANES, LANES)], sem.at[c])
        copy.start()
        copies.append(copy)
    for copy in copies:
        copy.wait()


def in_place(array):
    return pltpu.with_memory_space_constraint(array, pltpu.HBM)


def solution(mesh):
    lines, cols = mesh.shape["line"], mesh.shape["col"]

    def local(fields, viscosity):
        _, rows, deep, wide = fields.shape
        chunks = wide // LANES
        assert deep == 8 and 4 * chunks == lines
        f32 = jnp.float32
        tile = (8, LANES)
        vmem = pl.BlockSpec(memory_space=pltpu.VMEM)
        anywhere = pl.BlockSpec(memory_space=pl.ANY)
        dma = pltpu.SemaphoreType.DMA
        y, m, w, b = pl.pallas_call(
            functools.partial(main_kernel, lines, cols, rows, chunks),
            out_shape=(
                jax.ShapeDtypeStruct((4, chunks, rows) + tile, f32),
                jax.ShapeDtypeStruct((2, chunks, rows) + tile, f32),
                jax.ShapeDtypeStruct((2, chunks, rows) + tile, f32),
                jax.ShapeDtypeStruct((lines, 2) + tile, f32),
            ),
            in_specs=[anywhere, anywhere],
            out_specs=(vmem, vmem, vmem, vmem),
            scratch_shapes=[
                pltpu.VMEM((5, chunks, rows + 2) + tile, f32),
                pltpu.VMEM((4, chunks, rows) + tile, f32),
                pltpu.VMEM((2, chunks, rows) + tile, f32),
                pltpu.VMEM((2, chunks, 3) + tile, f32),
                pltpu.VMEM((2, chunks, 5, rows, LANES), f32),
                pltpu.VMEM((2, chunks, 5, rows, LANES), f32),
                pltpu.VMEM((chunks, 2, 3) + tile, f32),
                pltpu.VMEM((lines, 3) + tile, f32),
                pltpu.VMEM((lines, 2) + tile, f32),
                pltpu.VMEM((lines, 2) + tile, f32),
                pltpu.VMEM((lines + 1,) + tile, f32),
                pltpu.VMEM((lines, 2) + tile, f32),
                pltpu.VMEM((lines, 2) + tile, f32),
                dma((chunks, 2)),
                dma((2,)), dma((2,)), dma((2, chunks)), dma((2, chunks)),
                dma((lines,)), dma((lines,)), dma((lines,)), dma((lines,)), dma((lines,)), dma((lines,)),
                pltpu.SemaphoreType.REGULAR,
            ],
            compiler_params=pltpu.CompilerParams(
                collective_id=0, has_side_effects=True, vmem_limit_bytes=40 << 20
            ),
            name="eliminate",
        )(in_place(fields), in_place(viscosity))
        return pl.pallas_call(
            functools.partial(back_kernel, rows, chunks),
            out_shape=jax.ShapeDtypeStruct((4, rows, 8, wide), f32),
            in_specs=[vmem, vmem, vmem, vmem],
            out_specs=anywhere,
            scratch_shapes=[pltpu.VMEM((4, chunks, rows) + tile, f32), dma((chunks,))],
            compiler_params=pltpu.CompilerParams(vmem_limit_bytes=24 << 20),
            name="substitute",
        )(y, m, w, b)

    return jax.shard_map(
        local,
        mesh=mesh,
        in_specs=(P(None, "line", "col", None), P("line", "col", None)),
        out_specs=P(None, "line", "col", None),
        check_vma=False,
    )
```

time: 70.7 us -> 26.7 us (0.38)
  Pallas kernels: 0 us -> 26.5 us
  waiting for transfers between devices: 21.9 us -> 0 us
  starting transfers between devices: 21.5 us -> 0 us
  other arithmetic: 20.6 us -> 0 us
  local copies, waits for them, and re-layouts: 5.46 us -> 0 us
  between operations: 0.86 us -> 0.01 us
    pallas_call x0 -> x2, Pallas kernels: none -> 26.5 us  [the longest x1 24.6 us: local(): pl.pallas_call(functools.partial(main_kernel, lines, cols, rows, chunks),...]
    all_to_all x2 -> x0, waiting for transfers between devices: 15.8 us -> none  [the longest x1 8.68 us: local(): lax.all_to_all(blocks, 'line', split_axis=2, concat_axis=1, tiled=True)]
    all_to_all x2 -> x0, starting transfers between devices: 12.7 us -> none  [the longest x1 9.14 us: local(): lax.all_to_all(blocks, 'line', split_axis=2, concat_axis=1, tiled=True)]
    ppermute x4 -> x0, starting transfers between devices: 8.89 us -> none  [the longest x2 4.55 us: padded_2(): lax.ppermute(lax.slice_in_dim(block, block.shape[dim] - width, None, axis...]
    div x26 -> x0, other arithmetic: 8.21 us -> none  [the longest x10 5.83 us: cyclic_reduce(): (sources - sub_diag * source_prev - super_diag * source_next) / divisor]
    ppermute x4 -> x0, waiting for transfers between devices: 6.13 us -> none  [the longest x2 3.12 us: padded_2(): lax.ppermute(lax.slice_in_dim(block, block.shape[dim] - width, None, axis...]
    concatenate x8 -> x0, other arithmetic: 4.52 us -> none  [the longest x3 1.81 us: local(): stacked = jnp.concatenate([fields, viscosity[None]], axis=0)]
    sub x3 -> x0, other arithmetic: 3.22 us -> none  [the longest x1 2.99 us: local(): fields + scaling * (CROSS_RATE * along_y + CROSS_RATE * along_z)]
  transfers between devices with their start and end apart: 6 -> 0, of which waited for: 4 -> 0; matrix products, arithmetic and copies ran while one was open for 4% -> 0% of each run, Pallas kernels for 0% -> 0%
where the time goes in v1:
time: 26.7 us; the launch traced here: 26.6 us
  Pallas kernels  26.5 us (99%)
    pallas_call x1, Pallas kernels, local(): pl.pallas_call(functools.partial(main_kernel, lines, cols, rows, chunks),...  24.6 us
    pallas_call x1, Pallas kernels, local(): pl.pallas_call(functools.partial(back_kernel, rows, chunks), out_shape=ja...  1.95 us

profile of v1, /device:TPU:0, one launch (start us, length us, event | category | flops | bytes accessed | tf_op | source)
XLA Modules:
  0.0 26.6 jit_solution(9387970159015884294)
XLA Ops:
  0.0 24.6 %eliminate.1 = (f32[4,4,32,8,128]{4,3,2,1,0:T(8,128)S(1)}, f32[2,4,32,8,128]{4,3,2,1,0:T(8,128)S(1)}, f32[2,4,32,8,128]{4,3,2,1,0:T(8,128)S(1)}, f32[16,2,8,128]{3,2,1,0:T(8,128)S(1)}) custom-call(f32[4,32,8,512]{3,2,1,0:T(8,128)} %f_hbm.1, f32[32,8,512]{2,1,0:T(8,128)} %v_hbm.1), custom_call_target="tpu_custom_call" | custom-call | tf_op jit(solution)/shard_map/eliminate/pallas_call | solution.py:390
  24.6 2.0 %substitute.1 = f32[4,32,8,512]{3,2,1,0:T(8,128)} custom-call(f32[4,4,32,8,128]{4,3,2,1,0:T(8,128)S(1)} %get-tuple-element.9.y, f32[2,4,32,8,128]{4,3,2,1,0:T(8,128)S(1)} %get-tuple-element.10.m, f32[2,4,32,8,128]{4,3,2,1,0:T(8,128)S(1)} %get-tuple-element.11.w, f32[16,2,8,128]{3,2,1,0:T(8,128)S(1)} %get-tuple-element.12.b), custom_call_target="tpu_custom_call" | custom-call | tf_op jit(solution)/shard_map/substitute/pallas_call | solution.py:424

commit v2 on v1

v2 whole, which is shorter than its diff:
```python
import functools

import jax
import jax.numpy as jnp
from jax import lax
from jax.experimental import pallas as pl
from jax.experimental.pallas import tpu as pltpu
from jax.sharding import PartitionSpec as P

STIFF = 3072.0
THERMAL_RATIO = 0.8
CROSS_RATE = 0.2
ADVECTION = 0.25
BUOYANCY = 2.0
MESH = pl.DeviceIdType.MESH
LANES = 128
STEP = 6
SIDE = 4


def rates(q):
    return 0.5 * STIFF * (1.0 if q == 0 else THERMAL_RATIO)


def owner_of(c, a):
    near_x, near_y, high_x, high_y = c % 2, c // 2, a % 2, a // 2
    x = (2 + near_x) if high_x else (1 - near_x)
    y = (2 + near_y) if high_y else (1 - near_y)
    return y * SIDE + x


def slot_of(me):
    x, y = lax.rem(me, SIDE), me // SIDE
    high_x, high_y = x // 2, y // 2
    near_x = jnp.where(high_x == 1, x - 2, 1 - x)
    near_y = jnp.where(high_y == 1, y - 2, 1 - y)
    return near_x + 2 * near_y, high_x + 2 * high_y


def main_kernel(
    lines, cols, rows, chunks,
    f_hbm, v_hbm,
    u_out, y_end, m_end, w_end, b_out,
    fv, src, y_all, m_all, w_all, rec, mass, x_left, x_right, halo_in,
    mat_out, mat_in, rhs_out, rhs_in, sep, bounds, pivots,
    load_sem, x_send, x_recv, y_send, y_recv,
    mat_send, mat_recv, rhs_send, rhs_recv, sep_send, sep_recv, plane_sem,
):
    me = lax.axis_index("line")
    col = lax.axis_index("col")
    right, left = lax.rem(me + 1, lines), lax.rem(me + lines - 1, lines)
    above, below = lax.rem(col + 1, cols), lax.rem(col + cols - 1, cols)
    row_of, place = me // SIDE, lax.rem(me, SIDE)
    my_chunk, my_field = slot_of(me)
    my_slot = 4 * my_chunk + my_field
    last = rows - 1
    shape = (8, LANES)
    y_ref = [y_all.at[c] for c in range(chunks - 1)] + [y_end]
    m_ref = [m_all.at[c] for c in range(chunks - 1)] + [m_end]
    w_ref = [w_all.at[c] for c in range(chunks - 1)] + [w_end]

    barrier = pltpu.get_barrier_semaphore()
    row_peers = [row_of * SIDE + lax.rem(place + d, SIDE) for d in range(1, SIDE)]
    column_peers = [lax.rem(row_of + d, lines // SIDE) * SIDE + place for d in range(1, lines // SIDE)]
    greeted = [{"col": above}, {"col": below}]
    greeted += [{"line": p} for p in [right, left] + row_peers + column_peers]
    for peer in greeted:
        pl.semaphore_signal(barrier, inc=1, device_id=peer, device_id_type=MESH)

    loads = []
    own = pl.ds(1, rows)
    for c in range(chunks):
        lanes = pl.ds(c * LANES, LANES)
        loads.append(pltpu.make_async_copy(v_hbm.at[:, :, lanes], fv.at[4, c, own], load_sem.at[c, 0]))
    for c in range(chunks):
        lanes = pl.ds(c * LANES, LANES)
        loads.append(pltpu.make_async_copy(f_hbm.at[:, :, :, lanes], fv.at[pl.ds(0, 4), c, own], load_sem.at[c, 1]))
    for copy in loads:
        copy.start()

    pl.semaphore_wait(barrier, len(greeted))

    def x_copy(n, source, target, peer):
        return pltpu.make_async_remote_copy(
            source, target, x_send.at[n], x_recv.at[n], device_id={"line": peer}, device_id_type=MESH)

    x_copies = [
        x_copy(0, v_hbm.at[last], x_left.at[4], right),
        x_copy(1, f_hbm.at[:, last], x_left.at[pl.ds(0, 4)], right),
        x_copy(2, f_hbm.at[:, 0], x_right, left),
    ]
    for copy in x_copies:
        copy.start()
    y_copies = []
    for c in range(chunks):
        lanes = pl.ds(c * LANES, LANES)
        group = []
        for side, y, peer in ((0, 7, above), (1, 0, below)):
            for n, source, target in (
                (0, f_hbm.at[:, :, y, lanes], halo_in.at[side, c, pl.ds(0, 4)]),
                (1, v_hbm.at[:, y, lanes], halo_in.at[side, c, 4]),
            ):
                copy = pltpu.make_async_remote_copy(
                    source, target, y_send.at[side, c, n], y_recv.at[side, c, n],
                    device_id={"col": peer}, device_id_type=MESH)
                copy.start()
                group.append(copy)
        y_copies.append(group)
    for peer in column_peers:
        pl.semaphore_signal(plane_sem, inc=1, device_id={"line": peer}, device_id_type=MESH)

    for c in range(chunks):
        loads[c].wait()

    def matrix_row(c, q, k, a, h, e):
        r = 1.0 / (a + (h + e))
        m = a * r
        w = e * r
        rec[q, c, k] = r
        m_ref[c][q, k] = m
        w_ref[c][q, k] = w
        return m, w

    def matrix_step(i, carry):
        k = last - 1 - i
        new = []
        for c in range(chunks):
            total = fv[4, c, k + 1] + fv[4, c, k]
            for q in range(2):
                h, e, mass_right = carry[2 * c + q]
                m, w = matrix_row(c, q, k, rates(q) * total, h, e)
                new.append((1.0 + m * h, m * e, mass_right + w * h))
        return tuple(new)

    start = []
    for c in range(chunks):
        total = fv[4, c, rows] + fv[4, c, rows - 1]
        for q in range(2):
            a = rates(q) * total
            start.append((jnp.ones_like(a), a, jnp.zeros_like(a)))
    state = lax.fori_loop(0, last - 1, matrix_step, tuple(start))
    for c in range(chunks):
        for q in range(2):
            for n in range(3):
                mass[q, c, n] = state[2 * c + q][n]

    for c in range(chunks):
        loads[chunks + c].wait()
    lane = lax.broadcasted_iota(jnp.int32, shape, 1)
    level = lax.broadcasted_iota(jnp.int32, shape, 0)
    z_first, z_last = lane == 0, lane == LANES - 1
    y_first, y_last = level == 0, level == 7
    drift = 0.5 * ADVECTION
    inner_next = jnp.where(y_last, 0.0, drift)
    inner_prev = jnp.where(y_first, 0.0, drift)

    def source_row(p):
        half = 0.5 * CROSS_RATE
        zero = jnp.zeros(shape, jnp.float32)
        value = [[fv[a, c, p] if a < 4 else half * fv[4, c, p] for c in range(chunks)] for a in range(5)]
        ahead = [[pltpu.roll(x, LANES - 1, 1) for x in value[a]] + [zero] for a in range(5)]
        behind = [[zero] + [pltpu.roll(x, 1, 1) for x in value[a]] for a in range(5)]
        for c in range(chunks):

            def around(a):
                x = value[a][c]
                z_next = jnp.where(z_last, ahead[a][c + 1], ahead[a][c])
                z_prev = jnp.where(z_first, behind[a][c], behind[a][c + 1])
                return z_next, z_prev, pltpu.roll(x, 7, 0), pltpu.roll(x, 1, 0)

            v = value[4][c]
            z_next, z_prev, y_next, y_prev = around(4)
            face = [v + z_next, v + z_prev, jnp.where(y_last, 0.0, v + y_next), jnp.where(y_first, 0.0, v + y_prev)]
            around_all = (face[0] + face[1]) + (face[2] + face[3])
            speed_x = drift * value[0][c]
            speed_z = drift * value[2][c]
            speed = [-speed_z, speed_z, -(inner_next * value[1][c]), inner_prev * value[1][c]]
            weights = [[face[n] + speed[n] for n in range(4)], [THERMAL_RATIO * face[n] + speed[n] for n in range(4)]]
            centre = [1.0 - around_all, 1.0 - THERMAL_RATIO * around_all]
            for a in range(4):
                q = a // 3
                near = around(a)
                total = centre[q] * value[a][c] - speed_x * (fv[a, c, p + 1] - fv[a, c, p - 1])
                total += (weights[q][0] * near[0] + weights[q][1] * near[1]) + (
                    weights[q][2] * near[2] + weights[q][3] * near[3]
                )
                if a == 2:
                    total += BUOYANCY * value[3][c]
                src[a, c, p - 1] = total

    def source_step(p, nothing):
        source_row(p)
        return nothing

    lax.fori_loop(2, 2 + rows // 2, source_step, 0)

    x_copies[0].wait_recv()
    inside_left = jnp.where(me == 0, 0.0, 1.0)
    inside_right = jnp.where(me == lines - 1, 0.0, 1.0)
    for c in range(chunks):
        total = fv[4, c, 1] + inside_left * x_left[4, :, pl.ds(c * LANES, LANES)]
        wall = (1.0 - inside_right) * fv[4, c, rows]
        for q in range(2):
            h, e, mass_right = (mass[q, c, n] for n in range(3))
            m, w = matrix_row(c, q, 0, rates(q) * total, h, e)
            mat_out[c, q, 0] = m * e
            mat_out[c, q, 1] = m * h
            mat_out[c, q, 2] = 1.0 + mass_right + w * h + rates(q) * wall

    pl.semaphore_wait(plane_sem, len(column_peers))

    def mat_copy(c, a):
        return pltpu.make_async_remote_copy(
            mat_out.at[c, a // 3], mat_in.at[me], mat_send.at[4 * c + a], mat_recv.at[me],
            device_id={"line": owner_of(c, a)}, device_id_type=MESH)

    slots = [(c, a) for c in range(chunks) for a in range(4)]
    for c, a in slots:

        @pl.when(me != owner_of(c, a))
        def _(c=c, a=a):
            mat_copy(c, a).start()

    mat_in[me] = mat_out[my_chunk, my_field // 3]

    lax.fori_loop(2 + rows // 2, rows, source_step, 0)

    x_copies[1].wait_recv()
    x_copies[2].wait_recv()
    for c in range(chunks):
        lanes = pl.ds(c * LANES, LANES)
        for a in range(4):
            fv[a, c, 0] = inside_left * x_left[a, :, lanes]
            fv[a, c, rows + 1] = inside_right * x_right[a, :, lanes]
    source_row(1)
    source_row(rows)

    edge = jnp.where(y_first | y_last, 0.5 * CROSS_RATE, 0.0)
    sign = jnp.where(y_last, -drift, jnp.where(y_first, drift, 0.0))

    def rhs_copy(c, a):
        return pltpu.make_async_remote_copy(
            rhs_out.at[4 * c + a], rhs_in.at[me], rhs_send.at[4 * c + a], rhs_recv.at[me],
            device_id={"line": owner_of(c, a)}, device_id_type=MESH)

    for c in range(chunks):
        for copy in y_copies[c]:
            copy.wait_recv()

        def finished(k):
            def beyond(a):
                low = jnp.broadcast_to(halo_in[0, c, a, pl.ds(k, 1), :], shape)
                high = jnp.broadcast_to(halo_in[1, c, a, pl.ds(k, 1), :], shape)
                return jnp.where(y_last, high, low)

            face = edge * (fv[4, c, k + 1] + beyond(4))
            speed = sign * fv[1, c, k + 1]
            faces = (face, THERMAL_RATIO * face)
            weights = (faces[0] + speed, faces[1] + speed)
            out = []
            for a in range(4):
                q = a // 3
                out.append(src[a, c, k] + (weights[q] * beyond(a) - faces[q] * fv[a, c, k + 1]))
            return out

        def rhs_row(k, carry):
            given = finished(k)
            new = []
            for a in range(4):
                q = a // 3
                passed, gathered = carry[a]
                d = given[a] + passed
                y_ref[c][a, k] = rec[q, c, k] * d
                new.append((m_ref[c][q, k] * d, gathered + w_ref[c][q, k] * d))
            return tuple(new)

        def rhs_step(i, carry):
            for n in range(STEP):
                carry = rhs_row(last - 2 - STEP * i - n, carry)
            return carry

        at_last = finished(last)
        zero = jnp.zeros(shape, jnp.float32)
        ends = rhs_row(last - 1, tuple((zero, at_last[a]) for a in range(4)))
        assert (last - 1) % STEP == 0
        ends = lax.fori_loop(0, (last - 1) // STEP, rhs_step, ends)
        for a in range(4):
            rhs_out[4 * c + a, 0] = ends[a][0]
            rhs_out[4 * c + a, 1] = ends[a][1]

        for a in range(4):

            @pl.when(me != owner_of(c, a))
            def _(c=c, a=a):
                rhs_copy(c, a).start()

    rhs_in[me] = rhs_out[my_slot]

    def arrival(source, target, recv, j):
        return pltpu.make_async_remote_copy(
            source, target.at[j], rhs_send.at[0], recv.at[j], device_id={"line": left}, device_id_type=MESH)

    def mat_wait(d, nothing):
        arrival(mat_out.at[0, 0], mat_in, mat_recv, lax.rem(me + d, lines)).wait_recv()
        return nothing

    lax.fori_loop(1, lines, mat_wait, 0)

    def pivot_step(j, before):
        e = mat_in[j, 0]
        r = 1.0 / (e + before)
        m = e * r
        pivots[j, 0] = r
        pivots[j, 1] = m
        ahead = jnp.minimum(j + 1, lines - 1)
        own_mass = mat_in[j, 2] + jnp.where(j + 1 < lines, 1.0, 0.0) * mat_in[ahead, 1]
        return own_mass + m * before

    first = mat_in[0, 0] + (mat_in[0, 2] + mat_in[1, 1])
    final = lax.fori_loop(1, lines, pivot_step, first)
    final = 1.0 / final

    def rhs_wait(d, nothing):
        arrival(rhs_out.at[0], rhs_in, rhs_recv, lax.rem(me + d, lines)).wait_recv()
        return nothing

    lax.fori_loop(1, lines, rhs_wait, 0)
    given = [rhs_in[j, 1] + rhs_in[j + 1, 0] if j + 1 < lines else rhs_in[j, 1] for j in range(lines)]
    for j in range(1, lines):
        given[j] = given[j] + pivots[j, 1] * given[j - 1]
    value = final * given[lines - 1]
    sep[0] = jnp.zeros(shape, jnp.float32)
    sep[lines] = value
    for j in range(lines - 1, 0, -1):
        value = pivots[j, 0] * given[j - 1] + pivots[j, 1] * value
        sep[j] = value

    def sep_copy(j):
        return pltpu.make_async_remote_copy(
            sep.at[pl.ds(j, 2)], bounds.at[my_slot], sep_send.at[j], sep_recv.at[my_slot],
            device_id={"line": j}, device_id_type=MESH)

    for j in range(lines):

        @pl.when(me != j)
        def _(j=j):
            sep_copy(j).start()

    bounds[my_slot] = sep[pl.ds(me, 2)]

    for copy in x_copies + [copy for group in y_copies for copy in group]:
        copy.wait_send()
    for c, a in slots:

        @pl.when(me != owner_of(c, a))
        def _(c=c, a=a):
            mat_copy(c, a).wait_send()
            rhs_copy(c, a).wait_send()

    for c in range(chunks):
        for a in range(4):

            @pl.when(me != owner_of(c, a))
            def _(c=c, a=a):
                arrival(sep.at[pl.ds(0, 2)], bounds, sep_recv, 4 * c + a).wait_recv()

        if c < chunks - 1:
            substitute(
                last, y_ref[c], m_ref[c], w_ref[c],
                [(bounds[4 * c + a, 0], bounds[4 * c + a, 1]) for a in range(4)], u_out.at[c])
        else:
            for a in range(4):
                b_out[a] = bounds[4 * c + a]

    for j in range(lines):

        @pl.when(me != j)
        def _(j=j):
            sep_copy(j).wait_send()


def substitute(last, y, m, w, ends, out):
    def row(k, before):
        new = []
        for a in range(4):
            q = a // 3
            u = (y[a, k] + w[q, k] * ends[a][1]) + m[q, k] * before[a]
            out[a, k] = u
            new.append(u)
        return tuple(new)

    def step(i, before):
        for n in range(STEP):
            before = row(1 + STEP * i + n, before)
        return before

    assert (last - 1) % STEP == 0
    first = row(0, tuple(end[0] for end in ends))
    lax.fori_loop(0, (last - 1) // STEP, step, first)
    for a in range(4):
        out[a, last] = ends[a][1]


def back_kernel(rows, chunks, u, y, m, w, b, out, buf, sem):
    copies = []

    def write(c, source):
        copy = pltpu.make_async_copy(source, out.at[:, :, :, pl.ds(c * LANES, LANES)], sem.at[c])
        copy.start()
        copies.append(copy)

    for c in range(chunks - 1):
        write(c, u.at[c])
    substitute(rows - 1, y, m, w, [(b[a, 0], b[a, 1]) for a in range(4)], buf)
    write(chunks - 1, buf)
    for copy in copies:
        copy.wait()


def in_place(array):
    return pltpu.with_memory_space_constraint(array, pltpu.HBM)


def solution(mesh):
    lines, cols = mesh.shape["line"], mesh.shape["col"]

    def local(fields, viscosity):
        _, rows, deep, wide = fields.shape
        chunks = wide // LANES
        assert deep == 8 and 4 * chunks == lines
        f32 = jnp.float32
        tile = (8, LANES)
        vmem = pl.BlockSpec(memory_space=pltpu.VMEM)
        anywhere = pl.BlockSpec(memory_space=pl.ANY)
        dma = pltpu.SemaphoreType.DMA
        parts = pl.pallas_call(
            functools.partial(main_kernel, lines, cols, rows, chunks),
            out_shape=(
                jax.ShapeDtypeStruct((chunks - 1, 4, rows) + tile, f32),
                jax.ShapeDtypeStruct((4, rows) + tile, f32),
                jax.ShapeDtypeStruct((2, rows) + tile, f32),
                jax.ShapeDtypeStruct((2, rows) + tile, f32),
                jax.ShapeDtypeStruct((4, 2) + tile, f32),
            ),
            in_specs=[anywhere, anywhere],
            out_specs=(vmem,) * 5,
            scratch_shapes=[
                pltpu.VMEM((5, chunks, rows + 2) + tile, f32),
                pltpu.VMEM((4, chunks, rows) + tile, f32),
                pltpu.VMEM((chunks - 1, 4, rows) + tile, f32),
                pltpu.VMEM((chunks - 1, 2, rows) + tile, f32),
                pltpu.VMEM((chunks - 1, 2, rows) + tile, f32),
                pltpu.VMEM((2, chunks, rows) + tile, f32),
                pltpu.VMEM((2, chunks, 3) + tile, f32),
                pltpu.VMEM((5, deep, wide), f32),
                pltpu.VMEM((4, deep, wide), f32),
                pltpu.VMEM((2, chunks, 5, rows, LANES), f32),
                pltpu.VMEM((chunks, 2, 3) + tile, f32),
                pltpu.VMEM((lines, 3) + tile, f32),
                pltpu.VMEM((lines, 2) + tile, f32),
                pltpu.VMEM((lines, 2) + tile, f32),
                pltpu.VMEM((lines + 1,) + tile, f32),
                pltpu.VMEM((lines, 2) + tile, f32),
                pltpu.VMEM((lines, 2) + tile, f32),
                dma((chunks, 2)),
                dma((3,)), dma((3,)), dma((2, chunks, 2)), dma((2, chunks, 2)),
                dma((lines,)), dma((lines,)), dma((lines,)), dma((lines,)), dma((lines,)), dma((lines,)),
                pltpu.SemaphoreType.REGULAR,
            ],
            compiler_params=pltpu.CompilerParams(
                collective_id=0, has_side_effects=True, vmem_limit_bytes=40 << 20
            ),
            name="eliminate",
        )(in_place(fields), in_place(viscosity))
        return pl.pallas_call(
            functools.partial(back_kernel, rows, chunks),
            out_shape=jax.ShapeDtypeStruct((4, rows, 8, wide), f32),
            in_specs=[vmem] * 5,
            out_specs=anywhere,
            scratch_shapes=[pltpu.VMEM((4, rows) + tile, f32), dma((chunks,))],
            compiler_params=pltpu.CompilerParams(vmem_limit_bytes=24 << 20),
            name="substitute",
        )(*parts)

    return jax.shard_map(
        local,
        mesh=mesh,
        in_specs=(P(None, "line", "col", None), P("line", "col", None)),
        out_specs=P(None, "line", "col", None),
        check_vma=False,
    )
```

time: 26.7 us -> 26.6 us (level)
    pallas_call x1, Pallas kernels: 1.95 us -> 1.35 us  [local(): pl.pallas_call(functools.partial(back_kernel, rows, chunks), out_shape=ja...]
    pallas_call x1, Pallas kernels: 24.6 us -> 25.2 us  [local(): pl.pallas_call(functools.partial(main_kernel, lines, cols, rows, chunks),...]
where the time goes in v2:
time: 26.6 us; the launch traced here: 26.5 us
  Pallas kernels  26.5 us (100%)
    pallas_call x1, Pallas kernels, local(): pl.pallas_call(functools.partial(main_kernel, lines, cols, rows, chunks),...  25.2 us
    pallas_call x1, Pallas kernels, local(): pl.pallas_call(functools.partial(back_kernel, rows, chunks), out_shape=ja...  1.35 us

profile of v2, /device:TPU:0, one launch (start us, length us, event | category | flops | bytes accessed | tf_op | source)
XLA Modules:
  0.0 26.5 jit_solution(12013514284231121003)
XLA Ops:
  0.0 25.2 %eliminate.1 = (f32[3,4,32,8,128]{4,3,2,1,0:T(8,128)S(1)}, f32[4,32,8,128]{3,2,1,0:T(8,128)S(1)}, f32[2,32,8,128]{3,2,1,0:T(8,128)S(1)}, f32[2,32,8,128]{3,2,1,0:T(8,128)S(1)}, f32[4,2,8,128]{3,2,1,0:T(8,128)S(1)}) custom-call(f32[4,32,8,512]{3,2,1,0:T(8,128)} %f_hbm.1, f32[32,8,512]{2,1,0:T(8,128)} %v_hbm.1), custom_call_target="tpu_custom_call" | custom-call | tf_op jit(solution)/shard_map/eliminate/pallas_call | solution.py:436
  25.2 1.4 %substitute.1 = f32[4,32,8,512]{3,2,1,0:T(8,128)} custom-call(f32[3,4,32,8,128]{4,3,2,1,0:T(8,128)S(1)} %get-tuple-element.10.u, f32[4,32,8,128]{3,2,1,0:T(8,128)S(1)} %get-tuple-element.11.y, f32[2,32,8,128]{3,2,1,0:T(8,128)S(1)} %get-tuple-element.12.m, f32[2,32,8,128]{3,2,1,0:T(8,128)S(1)} %get-tuple-element.13.w, f32[4,2,8,128]{3,2,1,0:T(8,128)S(1)} %get-tuple-element.14.b), custom_call_target="tpu_custom_call" | custom-call | tf_op jit(solution)/shard_map/substitute/pallas_call | solution.py:475

commit v3 on v2

--- a/solution.py
+++ b/solution.py
@@ -14,7 +14,9 @@
 BUOYANCY = 2.0
 MESH = pl.DeviceIdType.MESH
 LANES = 128
-STEP = 6
+STEP = 15
+TRIP = 5
+EARLY = 2
 SIDE = 4
 
 
@@ -44,7 +46,7 @@
     fv, src, y_all, m_all, w_all, rec, mass, x_left, x_right, halo_in,
     mat_out, mat_in, rhs_out, rhs_in, sep, bounds, pivots,
     load_sem, x_send, x_recv, y_send, y_recv,
-    mat_send, mat_recv, rhs_send, rhs_recv, sep_send, sep_recv, plane_sem,
+    mat_send, mat_recv, rhs_send, rhs_recv, sep_send, sep_recv, plane_sem, ready_sem,
 ):
     me = lax.axis_index("line")
     col = lax.axis_index("col")
@@ -62,10 +64,15 @@
     barrier = pltpu.get_barrier_semaphore()
     row_peers = [row_of * SIDE + lax.rem(place + d, SIDE) for d in range(1, SIDE)]
     column_peers = [lax.rem(row_of + d, lines // SIDE) * SIDE + place for d in range(1, lines // SIDE)]
-    greeted = [{"col": above}, {"col": below}]
-    greeted += [{"line": p} for p in [right, left] + row_peers + column_peers]
+    greeted = [{"line": p} for p in [right, left] + row_peers + column_peers]
     for peer in greeted:
         pl.semaphore_signal(barrier, inc=1, device_id=peer, device_id_type=MESH)
+    odd = lax.rem(col, 2) == 1
+
+    @pl.when(jnp.logical_not(odd))
+    def _():
+        for peer in (above, below):
+            pl.semaphore_signal(barrier, inc=1, device_id={"col": peer}, device_id_type=MESH)
 
     loads = []
     own = pl.ds(1, rows)
@@ -78,36 +85,57 @@
     for copy in loads:
         copy.start()
 
-    pl.semaphore_wait(barrier, len(greeted))
+    @pl.when(odd)
+    def _():
+        pl.semaphore_wait(barrier, len(greeted) + 2)
+        for peer in (above, below):
+            pl.semaphore_signal(ready_sem, inc=1, device_id={"col": peer}, device_id_type=MESH)
+
+    @pl.when(jnp.logical_not(odd))
+    def _():
+        pl.semaphore_wait(barrier, len(greeted))
 
     def x_copy(n, source, target, peer):
         return pltpu.make_async_remote_copy(
             source, target, x_send.at[n], x_recv.at[n], device_id={"line": peer}, device_id_type=MESH)
 
-    x_copies = [
-        x_copy(0, v_hbm.at[last], x_left.at[4], right),
-        x_copy(1, f_hbm.at[:, last], x_left.at[pl.ds(0, 4)], right),
-        x_copy(2, f_hbm.at[:, 0], x_right, left),
-    ]
-    for copy in x_copies:
-        copy.start()
+    visc_copy = x_copy(0, v_hbm.at[last], x_left.at[4], right)
+    visc_copy.start()
+    x_copies = []
+    for c in range(chunks):
+        lanes = pl.ds(c * LANES, LANES)
+        x_copies.append((
+            x_copy(1 + c, f_hbm.at[:, last, :, lanes], x_left.at[pl.ds(0, 4), :, lanes], right),
+            x_copy(1 + chunks + c, f_hbm.at[:, 0, :, lanes], x_right.at[:, :, lanes], left),
+        ))
+        for copy in x_copies[c]:
+            copy.start()
     y_copies = []
     for c in range(chunks):
         lanes = pl.ds(c * LANES, LANES)
-        group = []
-        for side, y, peer in ((0, 7, above), (1, 0, below)):
+        y_copies.append([
+            pltpu.make_async_remote_copy(
+                source, target, y_send.at[side, c, n], y_recv.at[side, c, n],
+                device_id={"col": peer}, device_id_type=MESH)
+            for side, y, peer in ((0, 7, above), (1, 0, below))
             for n, source, target in (
                 (0, f_hbm.at[:, :, y, lanes], halo_in.at[side, c, pl.ds(0, 4)]),
                 (1, v_hbm.at[:, y, lanes], halo_in.at[side, c, 4]),
-            ):
-                copy = pltpu.make_async_remote_copy(
-                    source, target, y_send.at[side, c, n], y_recv.at[side, c, n],
-                    device_id={"col": peer}, device_id_type=MESH)
+            )
+        ])
+
+    def start_y():
+        for group in y_copies:
+            for copy in group:
                 copy.start()
-                group.append(copy)
-        y_copies.append(group)
+
+    pl.when(odd)(start_y)
     for peer in column_peers:
         pl.semaphore_signal(plane_sem, inc=1, device_id={"line": peer}, device_id_type=MESH)
+
+    for c in range(chunks):
+        fv[4, c, 0] = jnp.zeros(shape, jnp.float32)
+        fv[4, c, rows + 1] = jnp.zeros(shape, jnp.float32)
 
     for c in range(chunks):
         loads[c].wait()
@@ -151,50 +179,86 @@
     z_first, z_last = lane == 0, lane == LANES - 1
     y_first, y_last = level == 0, level == 7
     drift = 0.5 * ADVECTION
-    inner_next = jnp.where(y_last, 0.0, drift)
-    inner_prev = jnp.where(y_first, 0.0, drift)
-
-    def source_row(p):
-        half = 0.5 * CROSS_RATE
+    half_next, half_prev = (jnp.where(wall, 0.0, 0.5 * CROSS_RATE) for wall in (y_last, y_first))
+    inner_next, inner_prev = (jnp.where(wall, 0.0, drift) for wall in (y_last, y_first))
+
+    flat = fv.reshape(5 * chunks * (rows + 2) * 8, LANES)
+
+    half = 0.5 * CROSS_RATE
+
+    def source_z(p):
         zero = jnp.zeros(shape, jnp.float32)
-        value = [[fv[a, c, p] if a < 4 else half * fv[4, c, p] for c in range(chunks)] for a in range(5)]
-        ahead = [[pltpu.roll(x, LANES - 1, 1) for x in value[a]] + [zero] for a in range(5)]
-        behind = [[zero] + [pltpu.roll(x, 1, 1) for x in value[a]] for a in range(5)]
+
+        def around(values):
+            ahead = [pltpu.roll(x, LANES - 1, 1) for x in values] + [zero]
+            behind = [zero] + [pltpu.roll(x, 1, 1) for x in values]
+            z_next = [jnp.where(z_last, ahead[c + 1], ahead[c]) for c in range(chunks)]
+            z_prev = [jnp.where(z_first, behind[c], behind[c + 1]) for c in range(chunks)]
+            return z_next, z_prev
+
+        visc = [half * fv[4, c, p] for c in range(chunks)]
+        v_next, v_prev = around(visc)
+        face_next = [visc[c] + v_next[c] for c in range(chunks)]
+        face_prev = [visc[c] + v_prev[c] for c in range(chunks)]
+        speed = [drift * fv[2, c, p] for c in range(chunks)]
+        for q in range(2):
+            ratio = (1.0, THERMAL_RATIO)[q]
+            ahead, behind, centre = [], [], []
+            for c in range(chunks):
+                faces = [face_next[c], face_prev[c]] if q == 0 else [ratio * face_next[c], ratio * face_prev[c]]
+                ahead.append(faces[0] - speed[c])
+                behind.append(faces[1] + speed[c])
+                centre.append(1.0 - (faces[0] + faces[1]))
+            for a in ((0, 1, 2), (3,))[q]:
+                own = [fv[a, c, p] for c in range(chunks)]
+                z_next, z_prev = around(own)
+                for c in range(chunks):
+                    src[a, c, p - 1] = centre[c] * own[c] + (ahead[c] * z_next[c] + behind[c] * z_prev[c])
+
+    def source_xy(p):
         for c in range(chunks):
 
-            def around(a):
-                x = value[a][c]
-                z_next = jnp.where(z_last, ahead[a][c + 1], ahead[a][c])
-                z_prev = jnp.where(z_first, behind[a][c], behind[a][c + 1])
-                return z_next, z_prev, pltpu.roll(x, 7, 0), pltpu.roll(x, 1, 0)
-
-            v = value[4][c]
-            z_next, z_prev, y_next, y_prev = around(4)
-            face = [v + z_next, v + z_prev, jnp.where(y_last, 0.0, v + y_next), jnp.where(y_first, 0.0, v + y_prev)]
-            around_all = (face[0] + face[1]) + (face[2] + face[3])
-            speed_x = drift * value[0][c]
-            speed_z = drift * value[2][c]
-            speed = [-speed_z, speed_z, -(inner_next * value[1][c]), inner_prev * value[1][c]]
-            weights = [[face[n] + speed[n] for n in range(4)], [THERMAL_RATIO * face[n] + speed[n] for n in range(4)]]
-            centre = [1.0 - around_all, 1.0 - THERMAL_RATIO * around_all]
-            for a in range(4):
-                q = a // 3
-                near = around(a)
-                total = centre[q] * value[a][c] - speed_x * (fv[a, c, p + 1] - fv[a, c, p - 1])
-                total += (weights[q][0] * near[0] + weights[q][1] * near[1]) + (
-                    weights[q][2] * near[2] + weights[q][3] * near[3]
-                )
-                if a == 2:
-                    total += BUOYANCY * value[3][c]
-                src[a, c, p - 1] = total
-
-    def source_step(p, nothing):
-        source_row(p)
+            def level_pair(a):
+                at = ((a * chunks + c) * (rows + 2) + p) * 8
+                return flat[pl.ds(at + 1, 8), :], flat[pl.ds(at - 1, 8), :]
+
+            v = fv[4, c, p]
+            y_next, y_prev = level_pair(4)
+            face_next = half_next * (v + y_next)
+            face_prev = half_prev * (v + y_prev)
+            own = [fv[a, c, p] for a in range(4)]
+            speed_x = drift * own[0]
+            speed_next, speed_prev = inner_next * own[1], inner_prev * own[1]
+            for q in range(2):
+                if q == 1:
+                    face_next, face_prev = THERMAL_RATIO * face_next, THERMAL_RATIO * face_prev
+                ahead, behind, both = face_next - speed_next, face_prev + speed_prev, face_next + face_prev
+                for a in ((0, 1, 2), (3,))[q]:
+                    y_next, y_prev = level_pair(a)
+                    total = (ahead * y_next + behind * y_prev) - both * own[a]
+                    total -= speed_x * (fv[a, c, p + 1] - fv[a, c, p - 1])
+                    if a == 2:
+                        total += BUOYANCY * own[3]
+                    src[a, c, p - 1] += total
+
+    def source_step(i, nothing):
+        for n in range(TRIP):
+            source_z(2 + TRIP * i + n)
+        for n in range(TRIP):
+            source_xy(2 + TRIP * i + n)
         return nothing
 
-    lax.fori_loop(2, 2 + rows // 2, source_step, 0)
-
-    x_copies[0].wait_recv()
+    trips = (rows - 2) // TRIP
+    assert trips * TRIP == rows - 2
+
+    @pl.when(jnp.logical_not(odd))
+    def _():
+        pl.semaphore_wait(ready_sem, 2)
+        start_y()
+
+    lax.fori_loop(0, EARLY, source_step, 0)
+
+    visc_copy.wait_recv()
     inside_left = jnp.where(me == 0, 0.0, 1.0)
     inside_right = jnp.where(me == lines - 1, 0.0, 1.0)
     for c in range(chunks):
@@ -223,17 +287,19 @@
 
     mat_in[me] = mat_out[my_chunk, my_field // 3]
 
-    lax.fori_loop(2 + rows // 2, rows, source_step, 0)
-
-    x_copies[1].wait_recv()
-    x_copies[2].wait_recv()
-    for c in range(chunks):
+    lax.fori_loop(EARLY, trips, source_step, 0)
+    source_z(1)
+    source_z(rows)
+
+    for c in range(chunks):
+        for copy in x_copies[c]:
+            copy.wait_recv()
         lanes = pl.ds(c * LANES, LANES)
         for a in range(4):
             fv[a, c, 0] = inside_left * x_left[a, :, lanes]
             fv[a, c, rows + 1] = inside_right * x_right[a, :, lanes]
-    source_row(1)
-    source_row(rows)
+    source_xy(1)
+    source_xy(rows)
 
     edge = jnp.where(y_first | y_last, 0.5 * CROSS_RATE, 0.0)
     sign = jnp.where(y_last, -drift, jnp.where(y_first, drift, 0.0))
@@ -274,16 +340,11 @@
                 new.append((m_ref[c][q, k] * d, gathered + w_ref[c][q, k] * d))
             return tuple(new)
 
-        def rhs_step(i, carry):
-            for n in range(STEP):
-                carry = rhs_row(last - 2 - STEP * i - n, carry)
-            return carry
-
         at_last = finished(last)
         zero = jnp.zeros(shape, jnp.float32)
-        ends = rhs_row(last - 1, tuple((zero, at_last[a]) for a in range(4)))
-        assert (last - 1) % STEP == 0
-        ends = lax.fori_loop(0, (last - 1) // STEP, rhs_step, ends)
+        ends = tuple((zero, at_last[a]) for a in range(4))
+        for k in range(last - 1, -1, -1):
+            ends = rhs_row(k, ends)
         for a in range(4):
             rhs_out[4 * c + a, 0] = ends[a][0]
             rhs_out[4 * c + a, 1] = ends[a][1]
@@ -348,8 +409,10 @@
 
     bounds[my_slot] = sep[pl.ds(me, 2)]
 
-    for copy in x_copies + [copy for group in y_copies for copy in group]:
-        copy.wait_send()
+    visc_copy.wait_send()
+    for group in x_copies + y_copies:
+        for copy in group:
+            copy.wait_send()
     for c, a in slots:
 
         @pl.when(me != owner_of(c, a))
@@ -463,9 +526,9 @@
                 pltpu.VMEM((lines, 2) + tile, f32),
                 pltpu.VMEM((lines, 2) + tile, f32),
                 dma((chunks, 2)),
-                dma((3,)), dma((3,)), dma((2, chunks, 2)), dma((2, chunks, 2)),
+                dma((1 + 2 * chunks,)), dma((1 + 2 * chunks,)), dma((2, chunks, 2)), dma((2, chunks, 2)),
                 dma((lines,)), dma((lines,)), dma((lines,)), dma((lines,)), dma((lines,)), dma((lines,)),
-                pltpu.SemaphoreType.REGULAR,
+                pltpu.SemaphoreType.REGULAR, pltpu.SemaphoreType.REGULAR,
             ],
             compiler_params=pltpu.CompilerParams(
                 collective_id=0, has_side_effects=True, vmem_limit_bytes=40 << 20

time: 26.6 us -> 25.4 us (0.955)
  Pallas kernels: 26.5 us -> 25.3 us
    pallas_call x1, Pallas kernels: 25.2 us -> 24 us  [local(): pl.pallas_call(functools.partial(main_kernel, lines, cols, rows, chunks),...]
where the time goes in v3:
time: 25.4 us; the launch traced here: 25.3 us
  Pallas kernels  25.3 us (100%)
    pallas_call x1, Pallas kernels, local(): pl.pallas_call(functools.partial(main_kernel, lines, cols, rows, chunks),...  24 us
    pallas_call x1, Pallas kernels, local(): pl.pallas_call(functools.partial(back_kernel, rows, chunks), out_shape=ja...  1.35 us

profile of v3, /device:TPU:0, one launch (start us, length us, event | category | flops | bytes accessed | tf_op | source)
XLA Modules:
  0.0 25.3 jit_solution(17947437407121260183)
XLA Ops:
  0.0 24.0 %eliminate.1 = (f32[3,4,32,8,128]{4,3,2,1,0:T(8,128)S(1)}, f32[4,32,8,128]{3,2,1,0:T(8,128)S(1)}, f32[2,32,8,128]{3,2,1,0:T(8,128)S(1)}, f32[2,32,8,128]{3,2,1,0:T(8,128)S(1)}, f32[4,2,8,128]{3,2,1,0:T(8,128)S(1)}) custom-call(f32[4,32,8,512]{3,2,1,0:T(8,128)} %f_hbm.1, f32[32,8,512]{2,1,0:T(8,128)} %v_hbm.1), custom_call_target="tpu_custom_call" | custom-call | tf_op jit(solution)/shard_map/eliminate/pallas_call | solution.py:499
  24.0 1.4 %substitute.1 = f32[4,32,8,512]{3,2,1,0:T(8,128)} custom-call(f32[3,4,32,8,128]{4,3,2,1,0:T(8,128)S(1)} %get-tuple-element.10.u, f32[4,32,8,128]{3,2,1,0:T(8,128)S(1)} %get-tuple-element.11.y, f32[2,32,8,128]{3,2,1,0:T(8,128)S(1)} %get-tuple-element.12.m, f32[2,32,8,128]{3,2,1,0:T(8,128)S(1)} %get-tuple-element.13.w, f32[4,2,8,128]{3,2,1,0:T(8,128)S(1)} %get-tuple-element.14.b), custom_call_target="tpu_custom_call" | custom-call | tf_op jit(solution)/shard_map/substitute/pallas_call | solution.py:538

commit v4 on v3

--- a/solution.py
+++ b/solution.py
@@ -43,7 +43,7 @@
     lines, cols, rows, chunks,
     f_hbm, v_hbm,
     u_out, y_end, m_end, w_end, b_out,
-    fv, src, y_all, m_all, w_all, rec, mass, x_left, x_right, halo_in,
+    fv, src, y_all, m_all, w_all, rec, mass, x_left, x_right, halo_out, halo_in,
     mat_out, mat_in, rhs_out, rhs_in, sep, bounds, pivots,
     load_sem, x_send, x_recv, y_send, y_recv,
     mat_send, mat_recv, rhs_send, rhs_recv, sep_send, sep_recv, plane_sem, ready_sem,
@@ -82,8 +82,9 @@
     for c in range(chunks):
         lanes = pl.ds(c * LANES, LANES)
         loads.append(pltpu.make_async_copy(f_hbm.at[:, :, :, lanes], fv.at[pl.ds(0, 4), c, own], load_sem.at[c, 1]))
-    for copy in loads:
-        copy.start()
+    for c in range(chunks):
+        loads[c].start()
+        loads[chunks + c].start()
 
     @pl.when(odd)
     def _():
@@ -112,16 +113,11 @@
             copy.start()
     y_copies = []
     for c in range(chunks):
-        lanes = pl.ds(c * LANES, LANES)
         y_copies.append([
             pltpu.make_async_remote_copy(
-                source, target, y_send.at[side, c, n], y_recv.at[side, c, n],
+                halo_out.at[side, c], halo_in.at[side, c], y_send.at[side, c], y_recv.at[side, c],
                 device_id={"col": peer}, device_id_type=MESH)
-            for side, y, peer in ((0, 7, above), (1, 0, below))
-            for n, source, target in (
-                (0, f_hbm.at[:, :, y, lanes], halo_in.at[side, c, pl.ds(0, 4)]),
-                (1, v_hbm.at[:, y, lanes], halo_in.at[side, c, 4]),
-            )
+            for side, peer in ((0, above), (1, below))
         ])
 
     def start_y():
@@ -129,7 +125,6 @@
             for copy in group:
                 copy.start()
 
-    pl.when(odd)(start_y)
     for peer in column_peers:
         pl.semaphore_signal(plane_sem, inc=1, device_id={"line": peer}, device_id_type=MESH)
 
@@ -137,8 +132,16 @@
         fv[4, c, 0] = jnp.zeros(shape, jnp.float32)
         fv[4, c, rows + 1] = jnp.zeros(shape, jnp.float32)
 
+    flat = fv.reshape(5 * chunks * (rows + 2) * 8, LANES)
     for c in range(chunks):
         loads[c].wait()
+        loads[chunks + c].wait()
+        for a in range(5):
+            for side, y in ((0, 7), (1, 0)):
+                for g in range(0, rows, 8):
+                    at = ((a * chunks + c) * (rows + 2) + 1 + g) * 8 + y
+                    halo_out[side, c, a, g : g + 8, :] = flat[pl.ds(at, 8, stride=8), :]
+    pl.when(odd)(start_y)
 
     def matrix_row(c, q, k, a, h, e):
         r = 1.0 / (a + (h + e))
@@ -172,8 +175,6 @@
             for n in range(3):
                 mass[q, c, n] = state[2 * c + q][n]
 
-    for c in range(chunks):
-        loads[chunks + c].wait()
     lane = lax.broadcasted_iota(jnp.int32, shape, 1)
     level = lax.broadcasted_iota(jnp.int32, shape, 0)
     z_first, z_last = lane == 0, lane == LANES - 1
@@ -181,8 +182,6 @@
     drift = 0.5 * ADVECTION
     half_next, half_prev = (jnp.where(wall, 0.0, 0.5 * CROSS_RATE) for wall in (y_last, y_first))
     inner_next, inner_prev = (jnp.where(wall, 0.0, drift) for wall in (y_last, y_first))
-
-    flat = fv.reshape(5 * chunks * (rows + 2) * 8, LANES)
 
     half = 0.5 * CROSS_RATE
 
@@ -518,6 +517,7 @@
                 pltpu.VMEM((5, deep, wide), f32),
                 pltpu.VMEM((4, deep, wide), f32),
                 pltpu.VMEM((2, chunks, 5, rows, LANES), f32),
+                pltpu.VMEM((2, chunks, 5, rows, LANES), f32),
                 pltpu.VMEM((chunks, 2, 3) + tile, f32),
                 pltpu.VMEM((lines, 3) + tile, f32),
                 pltpu.VMEM((lines, 2) + tile, f32),
@@ -526,7 +526,7 @@
                 pltpu.VMEM((lines, 2) + tile, f32),
                 pltpu.VMEM((lines, 2) + tile, f32),
                 dma((chunks, 2)),
-                dma((1 + 2 * chunks,)), dma((1 + 2 * chunks,)), dma((2, chunks, 2)), dma((2, chunks, 2)),
+                dma((1 + 2 * chunks,)), dma((1 + 2 * chunks,)), dma((2, chunks)), dma((2, chunks)),
                 dma((lines,)), dma((lines,)), dma((lines,)), dma((lines,)), dma((lines,)), dma((lines,)),
                 pltpu.SemaphoreType.REGULAR, pltpu.SemaphoreType.REGULAR,
             ],

time: 25.4 us -> 25.2 us (level)
  no operation moved by 1% of the time
where the time goes in v4:
time: 25.2 us; the launch traced here: 25.1 us
  Pallas kernels  25.1 us (100%)
    pallas_call x1, Pallas kernels, local(): pl.pallas_call(functools.partial(main_kernel, lines, cols, rows, chunks),...  23.8 us
    pallas_call x1, Pallas kernels, local(): pl.pallas_call(functools.partial(back_kernel, rows, chunks), out_shape=ja...  1.35 us

profile of v4, /device:TPU:0, one launch (start us, length us, event | category | flops | bytes accessed | tf_op | source)
XLA Modules:
  0.0 25.1 jit_solution(15166897636120336271)
XLA Ops:
  0.0 23.8 %eliminate.1 = (f32[3,4,32,8,128]{4,3,2,1,0:T(8,128)S(1)}, f32[4,32,8,128]{3,2,1,0:T(8,128)S(1)}, f32[2,32,8,128]{3,2,1,0:T(8,128)S(1)}, f32[2,32,8,128]{3,2,1,0:T(8,128)S(1)}, f32[4,2,8,128]{3,2,1,0:T(8,128)S(1)}) custom-call(f32[4,32,8,512]{3,2,1,0:T(8,128)} %f_hbm.1, f32[32,8,512]{2,1,0:T(8,128)} %v_hbm.1), custom_call_target="tpu_custom_call" | custom-call | tf_op jit(solution)/shard_map/eliminate/pallas_call | solution.py:498
  23.8 1.4 %substitute.1 = f32[4,32,8,512]{3,2,1,0:T(8,128)} custom-call(f32[3,4,32,8,128]{4,3,2,1,0:T(8,128)S(1)} %get-tuple-element.10.u, f32[4,32,8,128]{3,2,1,0:T(8,128)S(1)} %get-tuple-element.11.y, f32[2,32,8,128]{3,2,1,0:T(8,128)S(1)} %get-tuple-element.12.m, f32[2,32,8,128]{3,2,1,0:T(8,128)S(1)} %get-tuple-element.13.w, f32[4,2,8,128]{3,2,1,0:T(8,128)S(1)} %get-tuple-element.14.b), custom_call_target="tpu_custom_call" | custom-call | tf_op jit(solution)/shard_map/substitute/pallas_call | solution.py:538

commit v5 on v4

--- a/solution.py
+++ b/solution.py
@@ -17,6 +17,7 @@
 STEP = 15
 TRIP = 5
 EARLY = 2
+SWAP = {2: 15, 15: 2}
 SIDE = 4
 
 
@@ -28,10 +29,13 @@
     near_x, near_y, high_x, high_y = c % 2, c // 2, a % 2, a // 2
     x = (2 + near_x) if high_x else (1 - near_x)
     y = (2 + near_y) if high_y else (1 - near_y)
-    return y * SIDE + x
+    return SWAP.get(y * SIDE + x, y * SIDE + x)
 
 
 def slot_of(me):
+    for one, other in SWAP.items():
+        if one < other:
+            me = jnp.where(me == one, other, jnp.where(me == other, one, me))
     x, y = lax.rem(me, SIDE), me // SIDE
     high_x, high_y = x // 2, y // 2
     near_x = jnp.where(high_x == 1, x - 2, 1 - x)
@@ -83,14 +87,14 @@
         lanes = pl.ds(c * LANES, LANES)
         loads.append(pltpu.make_async_copy(f_hbm.at[:, :, :, lanes], fv.at[pl.ds(0, 4), c, own], load_sem.at[c, 1]))
     for c in range(chunks):
-        loads[c].start()
-        loads[chunks + c].start()
+        loads[c].start(priority=1 if c == 0 else 0)
+        loads[chunks + c].start(priority=1 if c == 0 else 0)
 
     @pl.when(odd)
     def _():
         pl.semaphore_wait(barrier, len(greeted) + 2)
-        for peer in (above, below):
-            pl.semaphore_signal(ready_sem, inc=1, device_id={"col": peer}, device_id_type=MESH)
+        for side, peer in ((1, above), (0, below)):
+            pl.semaphore_signal(ready_sem.at[side], inc=1, device_id={"col": peer}, device_id_type=MESH)
 
     @pl.when(jnp.logical_not(odd))
     def _():
@@ -120,10 +124,12 @@
             for side, peer in ((0, above), (1, below))
         ])
 
-    def start_y():
+    def start_when_in(side):
+        pl.semaphore_wait(ready_sem.at[side], 1)
         for group in y_copies:
-            for copy in group:
-                copy.start()
+            group[side].start()
+
+    even, lowest = jnp.logical_not(odd), col == 0
 
     for peer in column_peers:
         pl.semaphore_signal(plane_sem, inc=1, device_id={"line": peer}, device_id_type=MESH)
@@ -141,7 +147,14 @@
                 for g in range(0, rows, 8):
                     at = ((a * chunks + c) * (rows + 2) + 1 + g) * 8 + y
                     halo_out[side, c, a, g : g + 8, :] = flat[pl.ds(at, 8, stride=8), :]
-    pl.when(odd)(start_y)
+
+        @pl.when(odd)
+        def _(c=c):
+            for copy in y_copies[c]:
+                copy.start()
+    pl.when(lowest)(lambda: start_when_in(0))
+    pl.when(even & jnp.logical_not(lowest))(lambda: start_when_in(1))
+
 
     def matrix_row(c, q, k, a, h, e):
         r = 1.0 / (a + (h + e))
@@ -214,8 +227,8 @@
                 for c in range(chunks):
                     src[a, c, p - 1] = centre[c] * own[c] + (ahead[c] * z_next[c] + behind[c] * z_prev[c])
 
-    def source_xy(p):
-        for c in range(chunks):
+    def source_xy(p, some):
+        for c in some:
 
             def level_pair(a):
                 at = ((a * chunks + c) * (rows + 2) + p) * 8
@@ -244,18 +257,15 @@
         for n in range(TRIP):
             source_z(2 + TRIP * i + n)
         for n in range(TRIP):
-            source_xy(2 + TRIP * i + n)
+            source_xy(2 + TRIP * i + n, range(chunks))
         return nothing
 
     trips = (rows - 2) // TRIP
     assert trips * TRIP == rows - 2
 
-    @pl.when(jnp.logical_not(odd))
-    def _():
-        pl.semaphore_wait(ready_sem, 2)
-        start_y()
-
     lax.fori_loop(0, EARLY, source_step, 0)
+    pl.when(lowest)(lambda: start_when_in(1))
+    pl.when(even & jnp.logical_not(lowest))(lambda: start_when_in(0))
 
     visc_copy.wait_recv()
     inside_left = jnp.where(me == 0, 0.0, 1.0)
@@ -289,16 +299,6 @@
     lax.fori_loop(EARLY, trips, source_step, 0)
     source_z(1)
     source_z(rows)
-
-    for c in range(chunks):
-        for copy in x_copies[c]:
-            copy.wait_recv()
-        lanes = pl.ds(c * LANES, LANES)
-        for a in range(4):
-            fv[a, c, 0] = inside_left * x_left[a, :, lanes]
-            fv[a, c, rows + 1] = inside_right * x_right[a, :, lanes]
-    source_xy(1)
-    source_xy(rows)
 
     edge = jnp.where(y_first | y_last, 0.5 * CROSS_RATE, 0.0)
     sign = jnp.where(y_last, -drift, jnp.where(y_first, drift, 0.0))
@@ -339,14 +339,24 @@
                 new.append((m_ref[c][q, k] * d, gathered + w_ref[c][q, k] * d))
             return tuple(new)
 
+        zero = jnp.zeros(shape, jnp.float32)
+        ends = ((zero, zero),) * 4
+        for k in range(last - 1, 0, -1):
+            ends = rhs_row(k, ends)
+
+        for copy in x_copies[c]:
+            copy.wait_recv()
+        lanes = pl.ds(c * LANES, LANES)
+        for a in range(4):
+            fv[a, c, 0] = inside_left * x_left[a, :, lanes]
+            fv[a, c, rows + 1] = inside_right * x_right[a, :, lanes]
+        source_xy(1, (c,))
+        source_xy(rows, (c,))
+        ends = rhs_row(0, ends)
         at_last = finished(last)
-        zero = jnp.zeros(shape, jnp.float32)
-        ends = tuple((zero, at_last[a]) for a in range(4))
-        for k in range(last - 1, -1, -1):
-            ends = rhs_row(k, ends)
         for a in range(4):
             rhs_out[4 * c + a, 0] = ends[a][0]
-            rhs_out[4 * c + a, 1] = ends[a][1]
+            rhs_out[4 * c + a, 1] = ends[a][1] + at_last[a]
 
         for a in range(4):
 
@@ -528,7 +538,7 @@
                 dma((chunks, 2)),
                 dma((1 + 2 * chunks,)), dma((1 + 2 * chunks,)), dma((2, chunks)), dma((2, chunks)),
                 dma((lines,)), dma((lines,)), dma((lines,)), dma((lines,)), dma((lines,)), dma((lines,)),
-                pltpu.SemaphoreType.REGULAR, pltpu.SemaphoreType.REGULAR,
+                pltpu.SemaphoreType.REGULAR, pltpu.SemaphoreType.REGULAR((2,)),
             ],
             compiler_params=pltpu.CompilerParams(
                 collective_id=0, has_side_effects=True, vmem_limit_bytes=40 << 20

time: 25.2 us -> 24.7 us (0.980)
  Pallas kernels: 25.1 us -> 24.6 us
    pallas_call x1, Pallas kernels: 23.8 us -> 23.2 us  [local(): pl.pallas_call(functools.partial(main_kernel, lines, cols, rows, chunks),...]
where the time goes in v5:
time: 24.7 us; the launch traced here: 24.6 us
  Pallas kernels  24.6 us (100%)
    pallas_call x1, Pallas kernels, local(): pl.pallas_call(functools.partial(main_kernel, lines, cols, rows, chunks),...  23.2 us
    pallas_call x1, Pallas kernels, local(): pl.pallas_call(functools.partial(back_kernel, rows, chunks), out_shape=ja...  1.35 us

profile of v5, /device:TPU:0, one launch (start us, length us, event | category | flops | bytes accessed | tf_op | source)
XLA Modules:
  0.0 24.6 jit_solution(15067917525572867657)
XLA Ops:
  0.0 23.2 %eliminate.1 = (f32[3,4,32,8,128]{4,3,2,1,0:T(8,128)S(1)}, f32[4,32,8,128]{3,2,1,0:T(8,128)S(1)}, f32[2,32,8,128]{3,2,1,0:T(8,128)S(1)}, f32[2,32,8,128]{3,2,1,0:T(8,128)S(1)}, f32[4,2,8,128]{3,2,1,0:T(8,128)S(1)}) custom-call(f32[4,32,8,512]{3,2,1,0:T(8,128)} %f_hbm.1, f32[32,8,512]{2,1,0:T(8,128)} %v_hbm.1), custom_call_target="tpu_custom_call" | custom-call | tf_op jit(solution)/shard_map/eliminate/pallas_call | solution.py:508
  23.2 1.4 %substitute.1 = f32[4,32,8,512]{3,2,1,0:T(8,128)} custom-call(f32[3,4,32,8,128]{4,3,2,1,0:T(8,128)S(1)} %get-tuple-element.10.u, f32[4,32,8,128]{3,2,1,0:T(8,128)S(1)} %get-tuple-element.11.y, f32[2,32,8,128]{3,2,1,0:T(8,128)S(1)} %get-tuple-element.12.m, f32[2,32,8,128]{3,2,1,0:T(8,128)S(1)} %get-tuple-element.13.w, f32[4,2,8,128]{3,2,1,0:T(8,128)S(1)} %get-tuple-element.14.b), custom_call_target="tpu_custom_call" | custom-call | tf_op jit(solution)/shard_map/substitute/pallas_call | solution.py:548

commit v6 on v5

--- a/solution.py
+++ b/solution.py
@@ -308,7 +308,19 @@
             rhs_out.at[4 * c + a], rhs_in.at[me], rhs_send.at[4 * c + a], rhs_recv.at[me],
             device_id={"line": owner_of(c, a)}, device_id_type=MESH)
 
-    for c in range(chunks):
+    def source_ends(c):
+        for copy in x_copies[c]:
+            copy.wait_recv()
+        lanes = pl.ds(c * LANES, LANES)
+        for a in range(4):
+            fv[a, c, 0] = inside_left * x_left[a, :, lanes]
+            fv[a, c, rows + 1] = inside_right * x_right[a, :, lanes]
+        source_xy(1, (c,))
+        source_xy(rows, (c,))
+
+    for c in range(chunks):
+        if c > 0:
+            source_ends(c)
         for copy in y_copies[c]:
             copy.wait_recv()
 
@@ -344,14 +356,8 @@
         for k in range(last - 1, 0, -1):
             ends = rhs_row(k, ends)
 
-        for copy in x_copies[c]:
-            copy.wait_recv()
-        lanes = pl.ds(c * LANES, LANES)
-        for a in range(4):
-            fv[a, c, 0] = inside_left * x_left[a, :, lanes]
-            fv[a, c, rows + 1] = inside_right * x_right[a, :, lanes]
-        source_xy(1, (c,))
-        source_xy(rows, (c,))
+        if c == 0:
+            source_ends(c)
         ends = rhs_row(0, ends)
         at_last = finished(last)
         for a in range(4):
@@ -390,11 +396,12 @@
     final = lax.fori_loop(1, lines, pivot_step, first)
     final = 1.0 / final
 
-    def rhs_wait(d, nothing):
-        arrival(rhs_out.at[0], rhs_in, rhs_recv, lax.rem(me + d, lines)).wait_recv()
-        return nothing
-
-    lax.fori_loop(1, lines, rhs_wait, 0)
+    for j in range(lines):
+
+        @pl.when(me != j)
+        def _(j=j):
+            arrival(rhs_out.at[0], rhs_in, rhs_recv, j).wait_recv()
+
     given = [rhs_in[j, 1] + rhs_in[j + 1, 0] if j + 1 < lines else rhs_in[j, 1] for j in range(lines)]
     for j in range(1, lines):
         given[j] = given[j] + pivots[j, 1] * given[j - 1]

time: 24.7 us -> 24.6 us (level)
  no operation moved by 1% of the time
where the time goes in v6:
time: 24.6 us; the launch traced here: 24.5 us
  Pallas kernels  24.5 us (100%)
    pallas_call x1, Pallas kernels, local(): pl.pallas_call(functools.partial(main_kernel, lines, cols, rows, chunks),...  23.2 us
    pallas_call x1, Pallas kernels, local(): pl.pallas_call(functools.partial(back_kernel, rows, chunks), out_shape=ja...  1.35 us

profile of v6, /device:TPU:0, one launch (start us, length us, event | category | flops | bytes accessed | tf_op | source)
XLA Modules:
  0.0 24.5 jit_solution(12024496669698521503)
XLA Ops:
  0.0 23.2 %eliminate.1 = (f32[3,4,32,8,128]{4,3,2,1,0:T(8,128)S(1)}, f32[4,32,8,128]{3,2,1,0:T(8,128)S(1)}, f32[2,32,8,128]{3,2,1,0:T(8,128)S(1)}, f32[2,32,8,128]{3,2,1,0:T(8,128)S(1)}, f32[4,2,8,128]{3,2,1,0:T(8,128)S(1)}) custom-call(f32[4,32,8,512]{3,2,1,0:T(8,128)} %f_hbm.1, f32[32,8,512]{2,1,0:T(8,128)} %v_hbm.1), custom_call_target="tpu_custom_call" | custom-call | tf_op jit(solution)/shard_map/eliminate/pallas_call | solution.py:515
  23.2 1.4 %substitute.1 = f32[4,32,8,512]{3,2,1,0:T(8,128)} custom-call(f32[3,4,32,8,128]{4,3,2,1,0:T(8,128)S(1)} %get-tuple-element.10.u, f32[4,32,8,128]{3,2,1,0:T(8,128)S(1)} %get-tuple-element.11.y, f32[2,32,8,128]{3,2,1,0:T(8,128)S(1)} %get-tuple-element.12.m, f32[2,32,8,128]{3,2,1,0:T(8,128)S(1)} %get-tuple-element.13.w, f32[4,2,8,128]{3,2,1,0:T(8,128)S(1)} %get-tuple-element.14.b), custom_call_target="tpu_custom_call" | custom-call | tf_op jit(solution)/shard_map/substitute/pallas_call | solution.py:555
